TPU v7x, 32 devices: a whole 2x2x4 slice. The times are simulated.
32 devices in a mesh: gx: 4 (over y, x), gy: 8 (over z, core).
Axes of the slice: x: 2, y: 2, z: 4, core: 2. Of those that a mesh axis runs over, the one named last changes fastest.
Arguments:
- parents: bfloat16 [256, 64, 256], P(('gx', 'gy')), may hold values from -6 to 6
- parent_dest: int32 [256], P(('gx', 'gy')), may hold values from -1 to 127, as said below
- skip: bfloat16 [256, 512, 128], P(('gx', 'gy')), may hold values from -6 to 6
- skip_dest: int32 [256], P(('gx', 'gy')), may hold values from -1 to 127, as said below
- neighbours: int32 [128, 26], P(('gx', 'gy')), may hold values from -1 to 127, as said below
- up_weight: bfloat16 [8, 256, 128], replicated, may hold values from -0.375 to 0.375
- conv_weight: bfloat16 [27, 256, 128], replicated, may hold values from -0.078125 to 0.078125
Outputs:
- refined: bfloat16 [128, 512, 128], P(('gx', 'gy'))
Inputs may be any that keep to these rules, and one draw needn't show every extreme that they name: `parent_dest`: each child brick index appears exactly once. Child brick c belongs to device c // 4 of the flattened axis gx+gy (gx slowest) and to its slot c % 4; it lies on a device with the same gx index as the slot that names it. One device names at most 1 child bricks of any one device, and in every draw some device names exactly 1 of one device. In every draw some device has all 8 of its slots live. `skip_dest`: each child brick index appears exactly once. Child brick c belongs to device c // 4 of the flattened axis gx+gy (gx slowest) and to its slot c % 4; it lies on a device with the same gx index as the slot that names it. One device names at most 1 child bricks of any one device, and in every draw some device names exactly 1 of one device. In every draw some device has all 8 of its slots live. Direction k = 0..25 enumerates (dx, dy, dz) in the finite set (-1,0,1)^3 with dx slowest and dz fastest, (0,0,0) left out. neighbours[c, k] is the child brick displaced from brick c by (dx, dy, dz) in the brick lattice, or -1 where no brick is there; the relation is symmetric. A brick's neighbours belong to its own device or to the devices just before and just after it on the flattened axis gx+gy.
All inputs are finite; a program needn't handle non-finite values.
Results may differ from a plain program's by a relative error of at most 0.0039.
Values may be sent and summed in bfloat16 or wider, within the bound.
A program may use at most 64 MiB of HBM per device.

v0:
```python
import functools

import jax
import jax.numpy as jnp
from jax import lax
from jax.experimental import pallas as pl
from jax.experimental.pallas import tpu as pltpu
from jax.sharding import PartitionSpec as P

neighbour_steps = [
    (code // 9 - 1, code // 3 % 3 - 1, code % 3 - 1) for code in range(27) if code != 13
]
direction_of = {step: k for k, step in enumerate(neighbour_steps)}
face_of = [
    (1 if x < 0 else 0) if x and not z else (5 if z < 0 else 4) if z else (3 if y < 0 else 2)
    for x, y, z in neighbour_steps
]
META = 8
VMEM_LIMIT = 60 * 2**20


def vmem():
    return pl.BlockSpec(memory_space=pltpu.VMEM)


def smem():
    return pl.BlockSpec(memory_space=pltpu.SMEM)


def anywhere():
    return pl.BlockSpec(memory_space=pl.ANY)


def pack_kernel(
    gy_count, bricks_dev, pdest, sdest, parents, skip, out_p, out_s, land, sem_p, sem_s
):
    slots, voxels = parents.shape[0], parents.shape[1]
    for d in range(gy_count):
        land[0, d] = -1
        land[1, d] = -1

    def copies(s):
        tp, ts = pdest[s], sdest[s]
        op = lax.rem(lax.div(jnp.maximum(tp, 0), bricks_dev), gy_count)
        os = lax.rem(lax.div(jnp.maximum(ts, 0), bricks_dev), gy_count)
        cp = pltpu.make_async_copy(parents.at[s], out_p.at[op, pl.ds(0, voxels)], sem_p.at[s])
        cs = pltpu.make_async_copy(skip.at[s], out_s.at[os], sem_s.at[s])
        return (tp, op, cp), (ts, os, cs)

    for s in range(slots):
        for which, (t, o, c) in enumerate(copies(s)):

            @pl.when(t >= 0)
            def _():
                land[which, o] = lax.rem(t, bricks_dev)
                c.start()

    for d in range(gy_count):
        half = parents.shape[2] // 2
        for which in range(2):
            mark = jnp.full((META, half), land[which, d], jnp.int32).astype(jnp.float32)
            out_p[d, voxels : voxels + META, which * half : (which + 1) * half] = mark.astype(
                jnp.bfloat16
            )
    for s in range(slots):
        for t, o, c in copies(s):

            @pl.when(t >= 0)
            def _():
                c.wait()


def pack(parent_dest, skip_dest, parents, skip, bricks_dev, gy_count):
    slots, voxels, channels = parents.shape
    return pl.pallas_call(
        functools.partial(pack_kernel, gy_count, bricks_dev),
        out_shape=(
            jax.ShapeDtypeStruct((gy_count, voxels + META, channels), parents.dtype),
            jax.ShapeDtypeStruct((gy_count,) + skip.shape[1:], skip.dtype),
        ),
        in_specs=[smem(), smem(), anywhere(), anywhere()],
        out_specs=(vmem(), vmem()),
        scratch_shapes=[
            pltpu.SMEM((2, gy_count), jnp.int32),
            pltpu.SemaphoreType.DMA((slots,)),
            pltpu.SemaphoreType.DMA((slots,)),
        ],
        compiler_params=pltpu.CompilerParams(vmem_limit_bytes=VMEM_LIMIT),
        name="pack",
    )(parent_dest, skip_dest, parents, skip)


def exchange_kernel(gy_count, in_p, in_s, out_p, out_s, sends, receives, own):
    me = lax.axis_index("gy")
    mine = [
        pltpu.make_async_copy(in_p.at[me], out_p.at[me], own.at[0]),
        pltpu.make_async_copy(in_s.at[me], out_s.at[me], own.at[1]),
    ]
    for copy in mine:
        copy.start()
    barrier = pltpu.get_barrier_semaphore()
    shifts = sorted(range(1, gy_count), key=lambda s: abs(s - gy_count // 2))
    for shift in shifts:
        pl.semaphore_signal(
            barrier,
            inc=1,
            device_id={"gy": lax.rem(me + shift, gy_count)},
            device_id_type=pl.DeviceIdType.MESH,
        )
    pl.semaphore_wait(barrier, gy_count - 1)
    copies = []
    for which, (source, landing) in enumerate(((in_p, out_p), (in_s, out_s))):
        for shift in shifts:
            there = lax.rem(me + shift, gy_count)
            copy = pltpu.make_async_remote_copy(
                src_ref=source.at[there],
                dst_ref=landing.at[me],
                send_sem=sends.at[which, shift],
                recv_sem=receives.at[which, shift],
                device_id={"gy": there},
                device_id_type=pl.DeviceIdType.MESH,
            )
            copy.start()
            copies.append(copy)
    for copy in copies:
        copy.wait()
    for copy in mine:
        copy.wait()


def exchange(in_p, in_s):
    gy_count = in_p.shape[0]
    return pl.pallas_call(
        functools.partial(exchange_kernel, gy_count),
        out_shape=tuple(jax.ShapeDtypeStruct(a.shape, a.dtype) for a in (in_p, in_s)),
        in_specs=[anywhere(), anywhere()],
        out_specs=(anywhere(), anywhere()),
        scratch_shapes=[
            pltpu.SemaphoreType.DMA((2, gy_count)),
            pltpu.SemaphoreType.DMA((2, gy_count)),
            pltpu.SemaphoreType.DMA((2,)),
        ],
        compiler_params=pltpu.CompilerParams(collective_id=0, has_side_effects=True),
        name="exchange",
    )(in_p, in_s)


def halo_kernel(size, inner, to_before, to_after, from_before, from_after, sends, receives):
    me = lax.axis_index("gx") * inner + lax.axis_index("gy")

    def coordinates(device):
        device = lax.max(device, 0)
        return (lax.div(device, inner), lax.rem(device, inner))

    ahead, behind = coordinates(me + 1), coordinates(me - 1)
    has_ahead, has_behind = me < size - 1, me > 0
    barrier = pltpu.get_barrier_semaphore()
    mesh_id = pl.DeviceIdType.MESH

    @pl.when(has_ahead)
    def _():
        pl.semaphore_signal(barrier, inc=1, device_id=ahead, device_id_type=mesh_id)

    @pl.when(has_behind)
    def _():
        pl.semaphore_signal(barrier, inc=1, device_id=behind, device_id_type=mesh_id)

    pl.semaphore_wait(barrier, has_ahead.astype(jnp.int32) + has_behind.astype(jnp.int32))
    up = pltpu.make_async_remote_copy(
        src_ref=to_after,
        dst_ref=from_before,
        send_sem=sends.at[0],
        recv_sem=receives.at[0],
        device_id=ahead,
        device_id_type=mesh_id,
    )
    down = pltpu.make_async_remote_copy(
        src_ref=to_before,
        dst_ref=from_after,
        send_sem=sends.at[1],
        recv_sem=receives.at[1],
        device_id=behind,
        device_id_type=mesh_id,
    )

    @pl.when(has_ahead)
    def _():
        up.start()

    @pl.when(has_behind)
    def _():
        down.start()

    @pl.when(has_ahead)
    def _():
        up.wait_send()
        down.wait_recv()

    @pl.when(has_behind)
    def _():
        down.wait_send()
        up.wait_recv()


def halo(to_before, to_after):
    inner = lax.axis_size("gy")
    size = lax.axis_size("gx") * inner
    return pl.pallas_call(
        functools.partial(halo_kernel, size, inner),
        out_shape=(
            jax.ShapeDtypeStruct(to_after.shape, to_after.dtype),
            jax.ShapeDtypeStruct(to_before.shape, to_before.dtype),
        ),
        in_specs=[anywhere(), anywhere()],
        out_specs=(anywhere(), anywhere()),
        scratch_shapes=[pltpu.SemaphoreType.DMA((2,)), pltpu.SemaphoreType.DMA((2,))],
        compiler_params=pltpu.CompilerParams(collective_id=1, has_side_effects=True),
        name="halo",
    )(to_before, to_after)


def build_kernel(
    source, near, pay, skip, up, feats, faces, before, after, spread, whole, sent
):
    channels = up.shape[1]
    made = up.shape[2]

    @pl.when(pl.program_id(0) == 0)
    def _():
        spread[...] = jnp.zeros_like(spread)

    for half in range(channels // 128):
        values = pay[0, 0:64, half * 128 : (half + 1) * 128].astype(jnp.float32)
        for c in range(2):
            spread[c * (channels // 128) + half, pl.ds(c, 64, stride=2), :] = values
    rows = jnp.concatenate([spread[p] for p in range(spread.shape[0])], axis=1).astype(jnp.bfloat16)
    for a in range(2):
        for b in range(2):
            tap = a * 4 + b * 2
            weight = jnp.concatenate([up[tap], up[tap + 1]], axis=0)
            value = jnp.dot(rows, weight, preferred_element_type=jnp.float32)
            for i in range(4):
                for j in range(4):
                    at = (2 * i + a) * 64 + (2 * j + b) * 8
                    for p in range(made // 128):
                        whole[p, at : at + 8] = value[
                            (i * 4 + j) * 8 : (i * 4 + j) * 8 + 8, p * 128 : (p + 1) * 128
                        ]
    for p in range(made // 128, whole.shape[0]):
        at = p * 128 - made
        whole[p] = skip[0, :, at : at + 128].astype(jnp.float32)
    for p in range(whole.shape[0]):
        lanes = slice(p * 128, (p + 1) * 128)
        feats[0, :, lanes] = whole[p].astype(jnp.bfloat16)
        for side in range(2):
            edge = 7 * side
            faces[0, side, :, lanes] = whole[p, edge * 64 : edge * 64 + 64].astype(jnp.bfloat16)
            faces[0, 2 + side, :, lanes] = jnp.concatenate(
                [whole[p, x * 64 + edge * 8 : x * 64 + edge * 8 + 8] for x in range(8)], axis=0
            ).astype(jnp.bfloat16)
            faces[0, 4 + side, :, lanes] = whole[p, pl.ds(edge, 64, stride=8), :].astype(
                jnp.bfloat16
            )
    brick = pl.program_id(0)
    count = before.shape[1]
    first = (lax.axis_index("gx") * lax.axis_size("gy") + lax.axis_index("gy")) * count
    for m in range(2 * count):
        sent[m] = 0
    for k, face in enumerate(face_of[::-1]):
        n = near[brick, k]
        off = n - first
        spot = jnp.where(off < 0, off + count, jnp.where(off >= count, off, 2 * count))
        sent[jnp.where(n >= 0, spot, 2 * count)] = face
    for m in range(count):
        before[0, m] = faces[0, sent[m]]
        after[0, m] = faces[0, sent[count + m]]


def build(source, near, pay, skip, up_weight, bricks_dev):
    channels, made = up_weight.shape[1:]
    joined = made + skip.shape[2]
    return pl.pallas_call(
        build_kernel,
        out_shape=(
            jax.ShapeDtypeStruct((bricks_dev, 512, joined), jnp.bfloat16),
            jax.ShapeDtypeStruct((bricks_dev, 6, 64, joined), jnp.bfloat16),
            jax.ShapeDtypeStruct((bricks_dev, bricks_dev, 64, joined), jnp.bfloat16),
            jax.ShapeDtypeStruct((bricks_dev, bricks_dev, 64, joined), jnp.bfloat16),
        ),
        grid_spec=pltpu.PrefetchScalarGridSpec(
            num_scalar_prefetch=2,
            grid=(bricks_dev,),
            in_specs=[
                pl.BlockSpec((1,) + pay.shape[1:], lambda b, s, t: (s[0, b], 0, 0)),
                pl.BlockSpec((1,) + skip.shape[1:], lambda b, s, t: (s[1, b], 0, 0)),
                pl.BlockSpec(up_weight.shape, lambda b, s, t: (0, 0, 0)),
            ],
            out_specs=(
                pl.BlockSpec((1, 512, joined), lambda b, s, t: (b, 0, 0)),
                pl.BlockSpec((1, 6, 64, joined), lambda b, s, t: (b, 0, 0, 0)),
                pl.BlockSpec((1, bricks_dev, 64, joined), lambda b, s, t: (b, 0, 0, 0)),
                pl.BlockSpec((1, bricks_dev, 64, joined), lambda b, s, t: (b, 0, 0, 0)),
            ),
            scratch_shapes=[
                pltpu.VMEM((2 * channels // 128, 128, 128), jnp.float32),
                pltpu.VMEM((joined // 128, 512, 128), jnp.float32),
                pltpu.SMEM((2 * bricks_dev + 1,), jnp.int32),
            ],
        ),
        compiler_params=pltpu.CompilerParams(vmem_limit_bytes=VMEM_LIMIT),
        name="build",
    )(source, near, pay, skip, up_weight)


def refine_kernel(
    near,
    feats,
    own,
    before,
    after,
    weight,
    out,
    pool,
    sems,
    body,
    plane,
    left,
    right,
    early,
    late,
):
    brick = pl.program_id(0)
    joined, made = weight.shape[1:]

    @pl.when(brick == 0)
    def _():
        copies, first = [], 0
        for i, part in enumerate((own, before, after)):
            length = part.shape[0]
            copies.append(pltpu.make_async_copy(part, pool.at[pl.ds(first, length)], sems.at[i]))
            copies[-1].start()
            first += length
        for tap in range(9):
            for dz in range(3):
                right[tap * joined : (tap + 1) * joined, dz * made : (dz + 1) * made] = weight[
                    tap * 3 + dz
                ]
        for copy in copies:
            copy.wait()

    count = pl.num_programs(0)
    first = (lax.axis_index("gx") * lax.axis_size("gy") + lax.axis_index("gy")) * count
    ahead = own.shape[0] + count * count + brick
    behind = before.shape[0] - 2 * count * count

    def taken(step, start, length):
        k = direction_of[step]
        n = near[brick, k]
        off = n - first
        spot = jnp.where(off < 0, ahead + off * count, ahead + behind + off * count)
        spot = jnp.where((off >= 0) & (off < count), off * 6 + face_of[k], spot)
        spot = jnp.where(n >= 0, spot, 0)
        low = start // 16 * 16
        high = -(-(start + length) // 16) * 16
        value = pool[spot, low:high, :].astype(jnp.float32)
        return jnp.where(n >= 0, value[start - low : start - low + length], 0.0)

    body[1:9, 1:9] = feats[0].astype(jnp.float32).reshape(8, 8, 8, joined)
    for ox in (-1, 1):
        u = 0 if ox < 0 else 9
        body[u, 1:9] = taken((ox, 0, 0), 0, 64).reshape(8, 8, joined)
        for oy in (-1, 1):
            v, ey = (0, 7) if oy < 0 else (9, 0)
            body[u, v] = taken((ox, oy, 0), ey * 8, 8)
    for oy in (-1, 1):
        v = 0 if oy < 0 else 9
        body[1:9, v] = taken((0, oy, 0), 0, 64).reshape(8, 8, joined)
    for p, oz in enumerate((-1, 1)):
        plane[p, 1:9, 1:9] = taken((0, 0, oz), 0, 64).reshape(8, 8, joined)
        for ox in (-1, 1):
            u, ex = (0, 7) if ox < 0 else (9, 0)
            plane[p, u, 1:9] = taken((ox, 0, oz), ex * 8, 8)
            for oy in (-1, 1):
                v, ey = (0, 7) if oy < 0 else (9, 0)
                row = taken((ox, oy, oz), ex * 8, 8)
                plane[p, u, v : v + 1] = row[ey : ey + 1]
        for oy in (-1, 1):
            v, ey = (0, 7) if oy < 0 else (9, 0)
            value = taken((0, oy, oz), 0, 64).reshape(8, 8, joined)
            plane[p, 1:9, v : v + 1] = value[:, ey : ey + 1]

    for tap in range(9):
        dx, dy = tap // 3, tap % 3
        lanes = slice(tap * joined, (tap + 1) * joined)
        left[0:512, lanes] = (
            body[dx : dx + 8, dy : dy + 8].reshape(512, joined).astype(jnp.bfloat16)
        )
        for p in range(2):
            left[512 + 64 * p : 576 + 64 * p, lanes] = (
                plane[p, dx : dx + 8, dy : dy + 8].reshape(64, joined).astype(jnp.bfloat16)
            )
    total = jnp.dot(left[...], right[...], preferred_element_type=jnp.float32)
    early[1:513] = total[0:512, 0:made]
    early[pl.ds(0, 64, stride=8), :] = total[512:576, 0:made]
    late[7:519] = total[0:512, 2 * made : 3 * made]
    late[pl.ds(15, 64, stride=8), :] = total[576:640, 2 * made : 3 * made]
    result = early[0:512] + total[0:512, made : 2 * made] + late[8:520]
    out[0] = jnp.maximum(result, 0.0).astype(jnp.bfloat16)


def refine(near, feats, own, before, after, conv_weight):
    bricks_dev, voxels, joined = feats.shape
    made = conv_weight.shape[2]
    return pl.pallas_call(
        refine_kernel,
        out_shape=jax.ShapeDtypeStruct((bricks_dev, voxels, made), jnp.bfloat16),
        grid_spec=pltpu.PrefetchScalarGridSpec(
            num_scalar_prefetch=1,
            grid=(bricks_dev,),
            in_specs=[
                pl.BlockSpec((1, voxels, joined), lambda b, s: (b, 0, 0)),
                anywhere(),
                anywhere(),
                anywhere(),
                pl.BlockSpec(conv_weight.shape, lambda b, s: (0, 0, 0)),
            ],
            out_specs=pl.BlockSpec((1, voxels, made), lambda b, s: (b, 0, 0)),
            scratch_shapes=[
                pltpu.VMEM((sum(a.shape[0] for a in (own, before, after)), 64, joined), own.dtype),
                pltpu.SemaphoreType.DMA((3,)),
                pltpu.VMEM((10, 10, 8, joined), jnp.float32),
                pltpu.VMEM((2, 10, 16, joined), jnp.float32),
                pltpu.VMEM((640, 9 * joined), jnp.bfloat16),
                pltpu.VMEM((9 * joined, 3 * made), jnp.bfloat16),
                pltpu.VMEM((520, made), jnp.float32),
                pltpu.VMEM((520, made), jnp.float32),
            ],
        ),
        compiler_params=pltpu.CompilerParams(vmem_limit_bytes=VMEM_LIMIT),
        name="refine",
    )(near, feats, own, before, after, conv_weight)


def per_device(parents, parent_dest, skip, skip_dest, neighbours, up_weight, conv_weight):
    bricks_dev = neighbours.shape[0]
    gy_count = lax.axis_size("gy")
    sent_p, sent_s = pack(parent_dest, skip_dest, parents, skip, bricks_dev, gy_count)
    came_p, came_s = exchange(sent_p, sent_s)
    voxels, channels = parents.shape[1:]
    spots = jnp.stack([came_p[:, voxels, 0], came_p[:, voxels, channels // 2]]).astype(jnp.int32)
    matches = spots[:, None, :] == jnp.arange(bricks_dev)[None, :, None]
    source = jnp.sum(jnp.where(matches, jnp.arange(gy_count)[None, None, :], 0), axis=2)
    feats, faces, to_before, to_after = build(
        source.astype(jnp.int32), neighbours, came_p, came_s, up_weight, bricks_dev
    )
    flat = (-1,) + faces.shape[2:]
    before, after = halo(to_before.reshape(flat), to_after.reshape(flat))
    return refine(neighbours, feats, faces.reshape(flat), before, after, conv_weight)


def solution(mesh):
    placed = (
        P(("gx", "gy"), None, None),
        P(("gx", "gy")),
        P(("gx", "gy"), None, None),
        P(("gx", "gy")),
        P(("gx", "gy"), None),
        P(),
        P(),
    )
    return jax.shard_map(
        per_device,
        mesh=mesh,
        in_specs=placed,
        out_specs=P(("gx", "gy"), None, None),
        check_vma=False,
    )
```

profile of v0, /device:TPU:1, one launch (start us, length us, event | category | flops | bytes accessed | tf_op | source)
XLA Modules:
  0.0 69.3 jit_solution(5297968820044038272)
XLA Ops:
  0.0 2.9 %pack.1 = (bf16[8,72,256]{2,1,0:T(8,128)(2,1)}, bf16[8,512,128]{2,1,0:T(8,128)(2,1)}) custom-call(s32[8]{0:T(128)} %pdest.1, s32[8]{0:T(128)} %sdest.1, bf16[8,64,256]{2,1,0:T(8,128)(2,1)} %parents.1, bf16[8,512,128]{2,1,0:T(8,128)(2,1)} %skip.1), custom_call_target="tpu_custom_call" | custom-call | tf_op jit(solution)/shard_map/pack/pallas_call | solution.py:75
  2.9 30.3 %exchange.1 = (bf16[8,72,256]{2,1,0:T(8,128)(2,1)}, bf16[8,512,128]{2,1,0:T(8,128)(2,1)}) custom-call(bf16[8,72,256]{2,1,0:T(8,128)(2,1)} %get-tuple-element.15.in_p, bf16[8,512,128]{2,1,0:T(8,128)(2,1)} %get-tuple-element.16.in_s), custom_call_target="tpu_custom_call" | custom-call | tf_op jit(solution)/shard_map/exchange/pallas_call | solution.py:133
  33.2 0.9 %slice_reduce_fusion.1 = (bf16[8]{0:T(256)(128)(2,1)S(1)}, bf16[8]{0:T(256)(128)(2,1)S(1)}) fusion(bf16[8,72,256]{2,1,0:T(8,128)(2,1)} %get-tuple-element.17.pay), kind=kLoop, calls=%fused_computation.3 | loop fusion | bytes 64 | tf_op jit(solution)/shard_map/slice | solution.py:450
  34.1 0.7 %select_reduce_fusion.source = s32[2,4]{1,0:T(2,128)} fusion(s32[2,8]{1,0:T(2,128)S(1)} %maximum_convert_fusion), kind=kLoop, calls=%fused_computation | loop fusion | flops 184 | bytes 96 | tf_op jit(solution)/shard_map/reduce_sum | solution.py:452
  34.8 5.2 %build.1 = (bf16[4,512,256]{2,1,0:T(8,128)(2,1)}, bf16[4,6,64,256]{3,2,1,0:T(8,128)(2,1)}, bf16[4,4,64,256]{3,2,1,0:T(8,128)(2,1)}, bf16[4,4,64,256]{3,2,1,0:T(8,128)(2,1)}) custom-call(s32[2,4]{1,0:T(2,128)} %select_reduce_fusion.source, s32[4,26]{1,0:T(4,128)} %near.3, bf16[8,72,256]{2,1,0:T(8,128)(2,1)} %get-tuple-element.17.pay, ...), custom_call_target="tpu_custom_call" | custom-call | tf_op jit(solution)/shard_map/build/pallas_call | solution.py:282
  40.0 17.9 %halo.1 = (bf16[16,64,256]{2,1,0:T(8,128)(2,1)}, bf16[16,64,256]{2,1,0:T(8,128)(2,1)}) custom-call(bf16[16,64,256]{2,1,0:T(8,128)(2,1)} %bitcast.6, bf16[16,64,256]{2,1,0:T(8,128)(2,1)} %bitcast.7), custom_call_target="tpu_custom_call" | custom-call | tf_op jit(solution)/shard_map/halo/pallas_call | solution.py:208
  57.9 11.4 %refine.1 = bf16[4,512,128]{2,1,0:T(8,128)(2,1)} custom-call(s32[4,26]{1,0:T(4,128)} %near.3, bf16[4,512,256]{2,1,0:T(8,128)(2,1)} %get-tuple-element.19.feats, bf16[24,64,256]{2,1,0:T(8,128)(2,1)} %bitcast.5, bf16[16,64,256]{2,1,0:T(8,128)(2,1)} %get-tuple-element.23.before, bf16[16,64,256]{2,1,0:T(8,128)(2,1)} %get-tuple-element.24.after, ...), custom_call_target="tpu_custom_call" | custom-call | tf_op jit(solution)/shard_map/refine/pallas_call | solution.py:414
  (1 shorter events, 0.0 us)
where the time goes:
time: 69.9 us; the launch traced here: 69.3 us
  Pallas kernels  67.6 us (97%)
  local copies, waits for them, and re-layouts  0.88 us (1%)
  other arithmetic  0.74 us (1%)
    pallas_call x1, Pallas kernels, exchange(): pl.pallas_call(functools.partial(exchange_kernel, gy_count), out_shape=tu...  30.3 us
    pallas_call x1, Pallas kernels, halo(): pl.pallas_call(functools.partial(halo_kernel, size, inner), out_shape=(ja...  17.9 us
    pallas_call x1, Pallas kernels, refine(): pl.pallas_call(refine_kernel, out_shape=jax.ShapeDtypeStruct((bricks_dev,...  11.4 us
    pallas_call x1, Pallas kernels, build(): pl.pallas_call(build_kernel, out_shape=(jax.ShapeDtypeStruct((bricks_dev,...  5.17 us
    pallas_call x1, Pallas kernels, pack(): pl.pallas_call(functools.partial(pack_kernel, gy_count, bricks_dev), out_...  2.86 us

commit v1 on v0

v1 whole, which is shorter than its diff:
```python
import functools

import jax
import jax.numpy as jnp
from jax import lax
from jax.experimental import pallas as pl
from jax.experimental.pallas import tpu as pltpu
from jax.sharding import PartitionSpec as P

steps = [(code // 9 - 1, code // 3 % 3 - 1, code % 3 - 1) for code in range(27) if code != 13]
direction_of = {step: k for k, step in enumerate(steps)}
face_of = [
    (1 if x < 0 else 0) if x and not z else (5 if z < 0 else 4) if z else (3 if y < 0 else 2)
    for x, y, z in steps
]
PITCH = 24
VMEM_LIMIT = 62 * 2**20
MESH = pl.DeviceIdType.MESH


def smem():
    return pl.BlockSpec(memory_space=pltpu.SMEM)


def anywhere():
    return pl.BlockSpec(memory_space=pl.ANY)


def partner(me, step):
    other, bit = me, 1
    while bit <= step:
        if step & bit:
            other = other + bit * (1 - 2 * lax.rem(lax.div(me, bit), 2))
        bit *= 2
    return other


def kernel(
    n_gx,
    n_gy,
    pdest,
    sdest,
    near,
    parents_hbm,
    skip_hbm,
    up_hbm,
    conv_hbm,
    out_hbm,
    parents,
    skip,
    up,
    conv,
    stage_p,
    stage_s,
    recv_p,
    recv_s,
    marks,
    land,
    face_pick,
    spots,
    spread,
    whole,
    ghost,
    own,
    pool_c,
    pool_s,
    halo_c,
    halo_s,
    body,
    even,
    odd,
    right,
    acc,
    result,
    loads,
    sends,
    receives,
    halo_sends,
    halo_receives,
    own_copy,
    outs,
):
    slots = parents.shape[0]
    count = near.shape[0]
    made = whole.shape[2]
    gx, me = lax.axis_index("gx"), lax.axis_index("gy")
    flat = gx * n_gy + me
    first = flat * count
    has_ahead, has_behind = flat < n_gx * n_gy - 1, flat > 0

    def coordinates(device):
        device = lax.max(device, 0)
        return (lax.div(device, n_gy), lax.rem(device, n_gy))

    ahead, behind = coordinates(flat + 1), coordinates(flat - 1)
    order = list(range(n_gy - 1, 0, -1))
    cross = [s for s in order if s >= n_gy // 2]
    rest = [s for s in order if s < n_gy // 2]

    load = [
        pltpu.make_async_copy(parents_hbm, parents, loads.at[0]),
        pltpu.make_async_copy(skip_hbm, skip, loads.at[1]),
        pltpu.make_async_copy(up_hbm, up, loads.at[2]),
        pltpu.make_async_copy(conv_hbm, conv, loads.at[3]),
    ]
    for copy in load:
        copy.start()

    barrier = pltpu.get_barrier_semaphore()
    wraps_ahead = has_ahead & (me == n_gy - 1)
    wraps_behind = has_behind & (me == 0)

    @pl.when(wraps_ahead)
    def _():
        pl.semaphore_signal(barrier, inc=1, device_id=ahead, device_id_type=MESH)

    @pl.when(wraps_behind)
    def _():
        pl.semaphore_signal(barrier, inc=1, device_id=behind, device_id_type=MESH)

    for step in order:
        pl.semaphore_signal(
            barrier, inc=1, device_id={"gy": partner(me, step)}, device_id_type=MESH
        )

    picks = []
    for which, dest in enumerate((pdest, sdest)):
        targets = [dest[s] for s in range(slots)]
        owners = [
            jnp.where(t >= 0, lax.rem(lax.div(lax.max(t, 0), count), n_gy), -1) for t in targets
        ]
        picked = []
        for d in range(n_gy):
            slot, mark = jnp.int32(0), jnp.int32(-1)
            for s in range(slots):
                here = owners[s] == d
                slot = jnp.where(here, s, slot)
                mark = jnp.where(here, targets[s], mark)
            marks[which * n_gy + d] = mark
            picked.append(slot)
        picks.append(picked)

    load[0].wait()
    for d in range(n_gy):
        stage_p[d] = parents[picks[0][d]]
    load[1].wait()
    for d in range(n_gy):
        stage_s[d] = skip[picks[1][d]]

    pl.semaphore_wait(
        barrier, n_gy - 1 + wraps_ahead.astype(jnp.int32) + wraps_behind.astype(jnp.int32)
    )

    def remote(source, landing, kind, step):
        return pltpu.make_async_remote_copy(
            src_ref=source,
            dst_ref=landing,
            send_sem=sends.at[kind, step],
            recv_sem=receives.at[kind, step],
            device_id={"gy": partner(me, step)},
            device_id_type=MESH,
        )

    mark_copies = [remote(marks, land.at[me], 0, s) for s in order]
    parent_copies = [remote(stage_p.at[partner(me, s)], recv_p.at[me], 1, s) for s in order]
    skip_copies = [remote(stage_s.at[partner(me, s)], recv_s.at[me], 2, s) for s in order]
    mine = [
        pltpu.make_async_copy(stage_p.at[me], recv_p.at[me], own_copy.at[0]),
        pltpu.make_async_copy(stage_s.at[me], recv_s.at[me], own_copy.at[1]),
    ]
    early = max(1, len(cross) // 2)
    for copy in mark_copies + parent_copies + skip_copies[:early] + mine:
        copy.start()
    for i in range(2 * n_gy):
        land[me, i] = marks[i]

    last = 6 * count + 2 * count * count

    def tables(b, carry):
        ids = [near[b, k] for k in range(26)]
        for m in range(2 * count):
            wanted = first - count + m if m < count else first + m
            face = jnp.int32(0)
            for k in range(26):
                face = jnp.where(ids[k] == wanted, face_of[25 - k], face)
            face_pick[b * 2 * count + m] = jnp.where(wanted < 0, 0, face)
        for k in range(26):
            off = ids[k] - first
            inside = (off >= 0) & (off < count)
            before = 6 * count + (off + count) * count + b
            after = 6 * count + off * count + b
            spot = jnp.where(inside, off * 6 + face_of[k], jnp.where(off < 0, before, after))
            spot = jnp.where(ids[k] >= 0, spot, last)
            spots[b * 26 + k] = lax.min(lax.max(spot, 0), last)
        return carry

    lax.fori_loop(0, count, tables, 0)

    for copy in load[2:]:
        copy.wait()
    zero = jnp.zeros((made, made), conv.dtype)
    for half in range(2):
        rows = slice(half * made, (half + 1) * made)
        for xx in range(4):
            for yz in range(9):
                at = (xx * 9 + yz) * made
                right[half, at : at + made, 0:made] = (
                    conv[xx * 9 + yz, rows, :] if xx < 3 else zero
                )
                right[half, at : at + made, made:] = (
                    conv[(xx - 1) * 9 + yz, rows, :] if xx > 0 else zero
                )
    for pool in (pool_c, pool_s):
        pool[last] = jnp.zeros(pool.shape[1:], pool.dtype)
    spread[...] = jnp.zeros_like(spread)

    for copy in mark_copies + parent_copies:
        copy.wait_recv()
    mine[0].wait()
    sources = []
    for which in range(2):
        held = [land[d, which * n_gy + me] for d in range(n_gy)]
        of = []
        for b in range(count):
            source = jnp.int32(0)
            for d in range(n_gy):
                source = jnp.where(held[d] == first + b, d, source)
            of.append(source)
        sources.append(of)

    def faces(b, pool):
        for f in range(6):
            edge = 7 * (f % 2)
            if f < 2:
                value = whole[b, edge * 64 : edge * 64 + 64]
            elif f < 4:
                value = jnp.concatenate(
                    [whole[b, x * 64 + edge * 8 : x * 64 + edge * 8 + 8] for x in range(8)], axis=0
                )
            else:
                value = whole[b, pl.ds(edge, 64, stride=8), :]
            value = value.astype(pool.dtype)
            own[b * 6 + f] = value
            pool[b * 6 + f] = value

    def send_halo(pool, halo, kind):
        for b in range(count):
            for m in range(count):
                halo[0, b * count + m] = own[b * 6 + face_pick[b * 2 * count + m]]
                halo[1, b * count + m] = own[b * 6 + face_pick[b * 2 * count + count + m]]
        own_faces, pairs = 6 * count, count * count
        down = pltpu.make_async_remote_copy(
            src_ref=halo.at[0],
            dst_ref=pool.at[pl.ds(own_faces + pairs, pairs)],
            send_sem=halo_sends.at[kind, 0],
            recv_sem=halo_receives.at[kind, 0],
            device_id=behind,
            device_id_type=MESH,
        )
        up_copy = pltpu.make_async_remote_copy(
            src_ref=halo.at[1],
            dst_ref=pool.at[pl.ds(own_faces, pairs)],
            send_sem=halo_sends.at[kind, 1],
            recv_sem=halo_receives.at[kind, 1],
            device_id=ahead,
            device_id_type=MESH,
        )

        @pl.when(has_ahead)
        def _():
            up_copy.start()

        @pl.when(has_behind)
        def _():
            down.start()

        return down, up_copy

    def wait_halo(copies):
        down, up_copy = copies

        @pl.when(has_ahead)
        def _():
            down.wait_recv()

        @pl.when(has_behind)
        def _():
            up_copy.wait_recv()

    def finish_halo(copies):
        down, up_copy = copies

        @pl.when(has_ahead)
        def _():
            up_copy.wait_send()

        @pl.when(has_behind)
        def _():
            down.wait_send()

    def upsample(b, source):
        for half in range(2):
            values = recv_p[source, :, half * 128 : (half + 1) * 128].astype(jnp.float32)
            for c in range(2):
                spread[c * 2 + half, pl.ds(c, 64, stride=2), :] = values
        rows = jnp.concatenate([spread[p] for p in range(4)], axis=1).astype(jnp.bfloat16)
        for a in range(2):
            for e in range(2):
                tap = a * 4 + e * 2
                weight = jnp.concatenate([up[tap], up[tap + 1]], axis=0)
                value = jnp.dot(rows, weight, preferred_element_type=jnp.float32)
                for i in range(4):
                    for j in range(4):
                        at = (2 * i + a) * 64 + (2 * j + e) * 8
                        whole[b, at : at + 8] = value[(i * 4 + j) * 8 : (i * 4 + j) * 8 + 8]

    for b in range(count):
        upsample(b, sources[0][b])
        faces(b, pool_c)
    halo_copies = send_halo(pool_c, halo_c, 0)
    for copy in skip_copies[early:]:
        copy.start()

    def pad(b, pool):
        def column(u, v):
            return (u * 10 + v) * PITCH

        def taken(step):
            return pool.at[spots[b * 26 + direction_of[step]]]

        def part(step, low, high):
            return taken(step)[low:high].astype(jnp.float32)

        for x in range(8):
            for y in range(8):
                at = column(x + 1, y + 1) + 8
                body[at : at + 8] = whole[b, x * 64 + y * 8 : x * 64 + y * 8 + 8]
        for ox in (-1, 1):
            u, ex = (0, 7) if ox < 0 else (9, 0)
            value = part((ox, 0, 0), 0, 64)
            for y in range(8):
                body[column(u, y + 1) + 8 : column(u, y + 1) + 16] = value[y * 8 : y * 8 + 8]
            for oy in (-1, 1):
                v, ey = (0, 7) if oy < 0 else (9, 0)
                low = ey * 8 // 16 * 16
                value = part((ox, oy, 0), low, low + 16)
                body[column(u, v) + 8 : column(u, v) + 16] = value[ey * 8 - low : ey * 8 - low + 8]
        for oy in (-1, 1):
            v = 0 if oy < 0 else 9
            value = part((0, oy, 0), 0, 64)
            for x in range(8):
                body[column(x + 1, v) + 8 : column(x + 1, v) + 16] = value[x * 8 : x * 8 + 8]
        for p, oz in enumerate((-1, 1)):
            z = 7 if oz < 0 else 16
            value = part((0, 0, oz), 0, 64)
            for x in range(8):
                body[pl.ds(column(x + 1, 1) + z, 8, stride=PITCH), :] = value[x * 8 : x * 8 + 8]
            for ox in (-1, 1):
                u, ex = (0, 7) if ox < 0 else (9, 0)
                low = ex * 8 // 16 * 16
                value = part((ox, 0, oz), low, low + 16)
                body[pl.ds(column(u, 1) + z, 8, stride=PITCH), :] = value[
                    ex * 8 - low : ex * 8 - low + 8
                ]
                for oy in (-1, 1):
                    v, ey = (0, 7) if oy < 0 else (9, 0)
                    value = part((ox, oy, oz), low, low + 16)
                    row = ex * 8 + ey - low
                    body[column(u, v) + z : column(u, v) + z + 1] = value[row : row + 1]
            for q, oy in enumerate((-1, 1)):
                v, ey = (0, 7) if oy < 0 else (9, 0)
                ghost[p * 2 + q] = part((0, oy, oz), 0, 64)
                body[pl.ds(column(1, v) + z, 8, stride=10 * PITCH), :] = ghost[
                    p * 2 + q, pl.ds(ey, 8, stride=8), :
                ]
        for dz in range(3):
            for u in range(10):
                blocks = [
                    body[column(u, v) + 7 + dz : column(u, v) + 15 + dz] for v in range(10)
                ]
                even[dz, u * 80 : u * 80 + 80] = jnp.concatenate(blocks, axis=0).astype(even.dtype)
                odd[dz, u * 64 : u * 64 + 64] = jnp.concatenate(blocks[1:9], axis=0).astype(
                    odd.dtype
                )

    def product(half):
        parts = []
        for xx in range(4):
            for dy in range(3):
                for dz in range(3):
                    if dy == 1:
                        rows = [odd[dz, (2 * s + xx) * 64 : (2 * s + xx) * 64 + 64] for s in range(4)]
                    else:
                        at = [(2 * s + xx) * 80 + dy * 8 for s in range(4)]
                        rows = [even[dz, a : a + 64] for a in at]
                    parts.append(jnp.concatenate(rows, axis=0))
        left = jnp.concatenate(parts, axis=1)
        return jnp.dot(left, right[half], preferred_element_type=jnp.float32)

    wait_halo(halo_copies)

    def child_half(b, carry):
        pad(b, pool_c)
        acc[b] = product(0)
        return carry

    lax.fori_loop(0, count, child_half, 0)

    for copy in skip_copies:
        copy.wait_recv()
    mine[1].wait()
    for b in range(count):
        whole[b] = recv_s[sources[1][b]].astype(jnp.float32)
        faces(b, pool_s)
    skip_halo = send_halo(pool_s, halo_s, 1)
    wait_halo(skip_halo)

    def skip_half(b, carry):
        pad(b, pool_s)
        total = jnp.maximum(acc[b] + product(1), 0.0).astype(result.dtype)
        for s in range(4):
            for p in range(2):
                at = (2 * s + p) * 64
                result[b, at : at + 64] = total[s * 64 : s * 64 + 64, p * made : (p + 1) * made]
        pltpu.make_async_copy(result.at[b], out_hbm.at[b], outs.at[b]).start()
        return carry

    lax.fori_loop(0, count, skip_half, 0)

    for copy in mark_copies + parent_copies + skip_copies:
        copy.wait_send()
    finish_halo(halo_copies)
    finish_halo(skip_halo)
    for b in range(count):
        pltpu.make_async_copy(result.at[b], out_hbm.at[b], outs.at[b]).wait()


def per_device(parents, parent_dest, skip, skip_dest, neighbours, up_weight, conv_weight):
    count = neighbours.shape[0]
    n_gx, n_gy = lax.axis_size("gx"), lax.axis_size("gy")
    voxels = skip.shape[1]
    made = conv_weight.shape[2]
    bf16, f32 = jnp.bfloat16, jnp.float32
    pool = (6 * count + 2 * count * count + 1, 64, made)
    dma = pltpu.SemaphoreType.DMA
    return pl.pallas_call(
        functools.partial(kernel, n_gx, n_gy),
        out_shape=jax.ShapeDtypeStruct((count, voxels, made), bf16),
        in_specs=[smem(), smem(), smem()] + [anywhere()] * 4,
        out_specs=anywhere(),
        scratch_shapes=[
            pltpu.VMEM(parents.shape, bf16),
            pltpu.VMEM(skip.shape, bf16),
            pltpu.VMEM(up_weight.shape, bf16),
            pltpu.VMEM(conv_weight.shape, bf16),
            pltpu.VMEM((n_gy,) + parents.shape[1:], bf16),
            pltpu.VMEM((n_gy,) + skip.shape[1:], bf16),
            pltpu.VMEM((n_gy,) + parents.shape[1:], bf16),
            pltpu.VMEM((n_gy,) + skip.shape[1:], bf16),
            pltpu.SMEM((2 * n_gy,), jnp.int32),
            pltpu.SMEM((n_gy, 2 * n_gy), jnp.int32),
            pltpu.SMEM((2 * count * count,), jnp.int32),
            pltpu.SMEM((26 * count,), jnp.int32),
            pltpu.VMEM((4, 128, 128), f32),
            pltpu.VMEM((count, voxels, made), f32),
            pltpu.VMEM((4, 64, made), f32),
            pltpu.VMEM((6 * count, 64, made), bf16),
            pltpu.VMEM(pool, bf16),
            pltpu.VMEM(pool, bf16),
            pltpu.VMEM((2, count * count, 64, made), bf16),
            pltpu.VMEM((2, count * count, 64, made), bf16),
            pltpu.VMEM((100 * PITCH, made), f32),
            pltpu.VMEM((3, 800, made), bf16),
            pltpu.VMEM((3, 640, made), bf16),
            pltpu.VMEM((2, 36 * made, 2 * made), bf16),
            pltpu.VMEM((count, voxels // 2, 2 * made), f32),
            pltpu.VMEM((count, voxels, made), bf16),
            dma((4,)),
            dma((3, n_gy)),
            dma((3, n_gy)),
            dma((2, 2)),
            dma((2, 2)),
            dma((2,)),
            dma((count,)),
        ],
        compiler_params=pltpu.CompilerParams(
            collective_id=0, has_side_effects=True, vmem_limit_bytes=VMEM_LIMIT
        ),
        name="refine_level",
    )(parent_dest, skip_dest, neighbours, parents, skip, up_weight, conv_weight)


def solution(mesh):
    placed = (
        P(("gx", "gy"), None, None),
        P(("gx", "gy")),
        P(("gx", "gy"), None, None),
        P(("gx", "gy")),
        P(("gx", "gy"), None),
        P(),
        P(),
    )
    return jax.shard_map(
        per_device,
        mesh=mesh,
        in_specs=placed,
        out_specs=P(("gx", "gy"), None, None),
        check_vma=False,
    )
```

time: 69.9 us -> 55.9 us (0.80)
  the two profiles are of different devices: /device:TPU:1 before, /device:TPU:4 now
where the time goes in v1:
time: 55.9 us; the launch traced here: 55.7 us
  Pallas kernels  53.8 us (96%)
  local copies, waits for them, and re-layouts  1.87 us (3%)
    pallas_call x1, Pallas kernels, per_device(): pl.pallas_call(functools.partial(kernel, n_gx, n_gy), out_shape=jax.Shape...  53.8 us
    unnamed x1, local copies, waits for them, and re-layouts  1.87 us

profile of v1, /device:TPU:4, one launch (start us, length us, event | category | flops | bytes accessed | tf_op | source)
XLA Modules:
  0.0 55.7 jit_solution(3641021385647613406)
XLA Ops:
  0.0 53.8 %refine_level.1 = bf16[4,512,128]{2,1,0:T(8,128)(2,1)} custom-call(s32[8]{0:T(128)} %pdest.1, s32[8]{0:T(128)} %sdest.1, s32[4,26]{1,0:T(4,128)} %near.1, bf16[8,64,256]{2,1,0:T(8,128)(2,1)} %parents_hbm.1, bf16[8,512,128]{2,1,0:T(8,128)(2,1)} %skip_hbm.1, bf16[8,256,128]{2,1,0:T(8,128)(2,1)} %up_hbm.1, bf16[27,256,128]{2,1,0:T(8,128)(2,1)} %conv_hbm.1), custom_call_target="tpu_custom_call" | custom-call | tf_op jit(solution)/shard_map/refine_level/pallas_call | solution.py:446
  53.8 1.9 %copy.9 = bf16[4,512,128]{2,1,0:T(8,128)(2,1)} copy(bf16[4,512,128]{2,1,0:T(8,128)(2,1)} %refine_level.1) | data formatting | bytes 1048576

commit v2 on v0

--- a/solution.py
+++ b/solution.py
@@ -7,28 +7,474 @@
 from jax.experimental.pallas import tpu as pltpu
 from jax.sharding import PartitionSpec as P
 
-neighbour_steps = [
-    (code // 9 - 1, code // 3 % 3 - 1, code % 3 - 1) for code in range(27) if code != 13
-]
-direction_of = {step: k for k, step in enumerate(neighbour_steps)}
+steps = [(code // 9 - 1, code // 3 % 3 - 1, code % 3 - 1) for code in range(27) if code != 13]
+direction_of = {step: k for k, step in enumerate(steps)}
 face_of = [
     (1 if x < 0 else 0) if x and not z else (5 if z < 0 else 4) if z else (3 if y < 0 else 2)
-    for x, y, z in neighbour_steps
+    for x, y, z in steps
 ]
+PITCH = 24
+VMEM_LIMIT = 62 * 2**20
+MESH = pl.DeviceIdType.MESH
+
+
+def smem():
+    return pl.BlockSpec(memory_space=pltpu.SMEM)
+
+
+def anywhere():
+    return pl.BlockSpec(memory_space=pl.ANY)
+
+
+def partner(me, step):
+    other, bit = me, 1
+    while bit <= step:
+        if step & bit:
+            other = other + bit * (1 - 2 * lax.rem(lax.div(me, bit), 2))
+        bit *= 2
+    return other
+
+
+def kernel(
+    n_gx,
+    n_gy,
+    pdest,
+    sdest,
+    near,
+    parents_hbm,
+    skip_hbm,
+    up_hbm,
+    conv_hbm,
+    out_hbm,
+    agreed,
+    parents,
+    skip,
+    up,
+    conv,
+    stage_p,
+    stage_s,
+    recv_p,
+    recv_s,
+    marks,
+    land,
+    agree,
+    agrees,
+    face_pick,
+    spots,
+    spread,
+    whole,
+    ghost,
+    own,
+    pool_c,
+    pool_s,
+    halo_c,
+    halo_s,
+    body,
+    even,
+    odd,
+    right,
+    acc,
+    result,
+    loads,
+    sends,
+    receives,
+    halo_sends,
+    halo_receives,
+    own_copy,
+    outs,
+    agree_sends,
+    agree_receives,
+):
+    slots = parents.shape[0]
+    count = near.shape[0]
+    made = whole.shape[2]
+    gx, me = lax.axis_index("gx"), lax.axis_index("gy")
+    flat = gx * n_gy + me
+    first = flat * count
+    has_ahead, has_behind = flat < n_gx * n_gy - 1, flat > 0
+
+    def coordinates(device):
+        device = lax.max(device, 0)
+        return (lax.div(device, n_gy), lax.rem(device, n_gy))
+
+    ahead, behind = coordinates(flat + 1), coordinates(flat - 1)
+    order = list(range(n_gy - 1, 0, -1))
+    cross = [s for s in order if s >= n_gy // 2]
+    rest = [s for s in order if s < n_gy // 2]
+
+    load = [
+        pltpu.make_async_copy(parents_hbm, parents, loads.at[0]),
+        pltpu.make_async_copy(skip_hbm, skip, loads.at[1]),
+        pltpu.make_async_copy(up_hbm, up, loads.at[2]),
+        pltpu.make_async_copy(conv_hbm, conv, loads.at[3]),
+    ]
+    for copy in load:
+        copy.start()
+
+    barrier = pltpu.get_barrier_semaphore()
+    wraps_ahead = has_ahead & (me == n_gy - 1)
+    wraps_behind = has_behind & (me == 0)
+
+    @pl.when(wraps_ahead)
+    def _():
+        pl.semaphore_signal(barrier, inc=1, device_id=ahead, device_id_type=MESH)
+
+    @pl.when(wraps_behind)
+    def _():
+        pl.semaphore_signal(barrier, inc=1, device_id=behind, device_id_type=MESH)
+
+    for step in order:
+        pl.semaphore_signal(
+            barrier, inc=1, device_id={"gy": partner(me, step)}, device_id_type=MESH
+        )
+
+    for step in range(1, n_gx):
+        pl.semaphore_signal(
+            barrier, inc=1, device_id={"gx": lax.rem(gx + step, n_gx)}, device_id_type=MESH
+        )
+
+    picks = []
+    for which, dest in enumerate((pdest, sdest)):
+        targets = [dest[s] for s in range(slots)]
+        owners = [
+            jnp.where(t >= 0, lax.rem(lax.div(lax.max(t, 0), count), n_gy), -1) for t in targets
+        ]
+        picked = []
+        for d in range(n_gy):
+            slot, mark = jnp.int32(0), jnp.int32(-1)
+            for s in range(slots):
+                here = owners[s] == d
+                slot = jnp.where(here, s, slot)
+                mark = jnp.where(here, targets[s], mark)
+            marks[which * n_gy + d] = mark
+            picked.append(slot)
+        picks.append(picked)
+
+    load[0].wait()
+    for d in range(n_gy):
+        stage_p[d] = parents[picks[0][d]]
+    load[1].wait()
+    for d in range(n_gy):
+        stage_s[d] = skip[picks[1][d]]
+
+    last = 8 * count
+
+    def tables(b, carry):
+        ids = [near[b, k] for k in range(26)]
+        offs = [i - first for i in ids]
+        enough = carry
+        for side in range(2):
+            low, high = jnp.int32(6), jnp.int32(-1)
+            for k in range(26):
+                off = offs[k] if side else offs[k] + 2 * count
+                there = (ids[k] >= 0) & (off >= count) & (off < 2 * count)
+                low = jnp.where(there, lax.min(low, face_of[25 - k]), low)
+                high = jnp.where(there, lax.max(high, face_of[25 - k]), high)
+            face_pick[b * 2 + side] = lax.max(high, 0)
+            enough = jnp.where((high >= 0) & (low != high), 0, enough)
+        for k in range(26):
+            off = offs[k]
+            inside = (off >= 0) & (off < count)
+            spot = jnp.where(inside, off * 6 + face_of[k], 6 * count + off)
+            spot = jnp.where(off < 0, 7 * count + off, spot)
+            spot = jnp.where(ids[k] >= 0, spot, last)
+            spots[b * 26 + k] = lax.min(lax.max(spot, 0), last)
+        return enough
+
+    marks[2 * n_gy] = lax.fori_loop(0, count, tables, jnp.int32(1))
+
+    pl.semaphore_wait(
+        barrier, n_gx + n_gy - 2 + wraps_ahead.astype(jnp.int32) + wraps_behind.astype(jnp.int32)
+    )
+
+    def remote(source, landing, kind, step):
+        return pltpu.make_async_remote_copy(
+            src_ref=source,
+            dst_ref=landing,
+            send_sem=sends.at[kind, step],
+            recv_sem=receives.at[kind, step],
+            device_id={"gy": partner(me, step)},
+            device_id_type=MESH,
+        )
+
+    mark_copies = [remote(marks, land.at[me], 0, s) for s in order]
+    parent_copies = [remote(stage_p.at[partner(me, s)], recv_p.at[me], 1, s) for s in order]
+    skip_copies = [remote(stage_s.at[partner(me, s)], recv_s.at[me], 2, s) for s in order]
+    mine = [
+        pltpu.make_async_copy(stage_p.at[me], recv_p.at[me], own_copy.at[0]),
+        pltpu.make_async_copy(stage_s.at[me], recv_s.at[me], own_copy.at[1]),
+    ]
+    early = max(1, len(cross) // 2)
+    for copy in mark_copies + parent_copies + skip_copies[:early] + mine:
+        copy.start()
+    for i in range(2 * n_gy + 1):
+        land[me, i] = marks[i]
+
+    for copy in load[2:]:
+        copy.wait()
+    zero = jnp.zeros((made, made), conv.dtype)
+    for half in range(2):
+        rows = slice(half * made, (half + 1) * made)
+        for xx in range(4):
+            for yz in range(9):
+                at = (xx * 9 + yz) * made
+                right[half, at : at + made, 0:made] = (
+                    conv[xx * 9 + yz, rows, :] if xx < 3 else zero
+                )
+                right[half, at : at + made, made:] = (
+                    conv[(xx - 1) * 9 + yz, rows, :] if xx > 0 else zero
+                )
+    for pool in (pool_c, pool_s):
+        pool[last] = jnp.zeros(pool.shape[1:], pool.dtype)
+    spread[...] = jnp.zeros_like(spread)
+
+    for copy in mark_copies + parent_copies:
+        copy.wait_recv()
+    mine[0].wait()
+    enough = land[0, 2 * n_gy]
+    for d in range(1, n_gy):
+        enough = lax.min(enough, land[d, 2 * n_gy])
+    agree[0] = enough
+    agrees[gx, 0] = enough
+    agree_copies = [
+        pltpu.make_async_remote_copy(
+            src_ref=agree,
+            dst_ref=agrees.at[gx],
+            send_sem=agree_sends.at[step],
+            recv_sem=agree_receives.at[step],
+            device_id={"gx": lax.rem(gx + step, n_gx)},
+            device_id_type=MESH,
+        )
+        for step in range(1, n_gx)
+    ]
+    for copy in agree_copies:
+        copy.start()
+    sources = []
+    for which in range(2):
+        held = [land[d, which * n_gy + me] for d in range(n_gy)]
+        of = []
+        for b in range(count):
+            source = jnp.int32(0)
+            for d in range(n_gy):
+                source = jnp.where(held[d] == first + b, d, source)
+            of.append(source)
+        sources.append(of)
+
+    def faces(b, pool):
+        for f in range(6):
+            edge = 7 * (f % 2)
+            if f < 2:
+                value = whole[b, edge * 64 : edge * 64 + 64]
+            elif f < 4:
+                value = jnp.concatenate(
+                    [whole[b, x * 64 + edge * 8 : x * 64 + edge * 8 + 8] for x in range(8)], axis=0
+                )
+            else:
+                value = whole[b, pl.ds(edge, 64, stride=8), :]
+            value = value.astype(pool.dtype)
+            own[b * 6 + f] = value
+            pool[b * 6 + f] = value
+
+    def send_halo(pool, halo, kind):
+        for b in range(count):
+            for side in range(2):
+                halo[side, b] = own[b * 6 + face_pick[b * 2 + side]]
+        down = pltpu.make_async_remote_copy(
+            src_ref=halo.at[0],
+            dst_ref=pool.at[pl.ds(7 * count, count)],
+            send_sem=halo_sends.at[kind, 0],
+            recv_sem=halo_receives.at[kind, 0],
+            device_id=behind,
+            device_id_type=MESH,
+        )
+        up_copy = pltpu.make_async_remote_copy(
+            src_ref=halo.at[1],
+            dst_ref=pool.at[pl.ds(6 * count, count)],
+            send_sem=halo_sends.at[kind, 1],
+            recv_sem=halo_receives.at[kind, 1],
+            device_id=ahead,
+            device_id_type=MESH,
+        )
+
+        @pl.when(has_ahead)
+        def _():
+            up_copy.start()
+
+        @pl.when(has_behind)
+        def _():
+            down.start()
+
+        return down, up_copy
+
+    def wait_halo(copies):
+        down, up_copy = copies
+
+        @pl.when(has_ahead)
+        def _():
+            down.wait_recv()
+
+        @pl.when(has_behind)
+        def _():
+            up_copy.wait_recv()
+
+    def finish_halo(copies):
+        down, up_copy = copies
+
+        @pl.when(has_ahead)
+        def _():
+            up_copy.wait_send()
+
+        @pl.when(has_behind)
+        def _():
+            down.wait_send()
+
+    def upsample(b, source):
+        for half in range(2):
+            values = recv_p[source, :, half * 128 : (half + 1) * 128].astype(jnp.float32)
+            for c in range(2):
+                spread[c * 2 + half, pl.ds(c, 64, stride=2), :] = values
+        rows = jnp.concatenate([spread[p] for p in range(4)], axis=1).astype(jnp.bfloat16)
+        for a in range(2):
+            for e in range(2):
+                tap = a * 4 + e * 2
+                weight = jnp.concatenate([up[tap], up[tap + 1]], axis=0)
+                value = jnp.dot(rows, weight, preferred_element_type=jnp.float32)
+                for i in range(4):
+                    for j in range(4):
+                        at = (2 * i + a) * 64 + (2 * j + e) * 8
+                        whole[b, at : at + 8] = value[(i * 4 + j) * 8 : (i * 4 + j) * 8 + 8]
+
+    for b in range(count):
+        upsample(b, sources[0][b])
+        faces(b, pool_c)
+    halo_copies = send_halo(pool_c, halo_c, 0)
+    for copy in skip_copies[early:]:
+        copy.start()
+
+    def pad(b, pool):
+        def column(u, v):
+            return (u * 10 + v) * PITCH
+
+        def taken(step):
+            return pool.at[spots[b * 26 + direction_of[step]]]
+
+        def part(step, low, high):
+            return taken(step)[low:high].astype(jnp.float32)
+
+        for x in range(8):
+            for y in range(8):
+                at = column(x + 1, y + 1) + 8
+                body[at : at + 8] = whole[b, x * 64 + y * 8 : x * 64 + y * 8 + 8]
+        for ox in (-1, 1):
+            u, ex = (0, 7) if ox < 0 else (9, 0)
+            value = part((ox, 0, 0), 0, 64)
+            for y in range(8):
+                body[column(u, y + 1) + 8 : column(u, y + 1) + 16] = value[y * 8 : y * 8 + 8]
+            for oy in (-1, 1):
+                v, ey = (0, 7) if oy < 0 else (9, 0)
+                low = ey * 8 // 16 * 16
+                value = part((ox, oy, 0), low, low + 16)
+                body[column(u, v) + 8 : column(u, v) + 16] = value[ey * 8 - low : ey * 8 - low + 8]
+        for oy in (-1, 1):
+            v = 0 if oy < 0 else 9
+            value = part((0, oy, 0), 0, 64)
+            for x in range(8):
+                body[column(x + 1, v) + 8 : column(x + 1, v) + 16] = value[x * 8 : x * 8 + 8]
+        for p, oz in enumerate((-1, 1)):
+            z = 7 if oz < 0 else 16
+            value = part((0, 0, oz), 0, 64)
+            for x in range(8):
+                body[pl.ds(column(x + 1, 1) + z, 8, stride=PITCH), :] = value[x * 8 : x * 8 + 8]
+            for ox in (-1, 1):
+                u, ex = (0, 7) if ox < 0 else (9, 0)
+                low = ex * 8 // 16 * 16
+                value = part((ox, 0, oz), low, low + 16)
+                body[pl.ds(column(u, 1) + z, 8, stride=PITCH), :] = value[
+                    ex * 8 - low : ex * 8 - low + 8
+                ]
+                for oy in (-1, 1):
+                    v, ey = (0, 7) if oy < 0 else (9, 0)
+                    value = part((ox, oy, oz), low, low + 16)
+                    row = ex * 8 + ey - low
+                    body[column(u, v) + z : column(u, v) + z + 1] = value[row : row + 1]
+            for q, oy in enumerate((-1, 1)):
+                v, ey = (0, 7) if oy < 0 else (9, 0)
+                ghost[p * 2 + q] = part((0, oy, oz), 0, 64)
+                body[pl.ds(column(1, v) + z, 8, stride=10 * PITCH), :] = ghost[
+                    p * 2 + q, pl.ds(ey, 8, stride=8), :
+                ]
+        for dz in range(3):
+            for u in range(10):
+                blocks = [
+                    body[column(u, v) + 7 + dz : column(u, v) + 15 + dz] for v in range(10)
+                ]
+                even[dz, u * 80 : u * 80 + 80] = jnp.concatenate(blocks, axis=0).astype(even.dtype)
+                odd[dz, u * 64 : u * 64 + 64] = jnp.concatenate(blocks[1:9], axis=0).astype(
+                    odd.dtype
+                )
+
+    def product(half):
+        parts = []
+        for xx in range(4):
+            for dy in range(3):
+                for dz in range(3):
+                    if dy == 1:
+                        rows = [odd[dz, (2 * s + xx) * 64 : (2 * s + xx) * 64 + 64] for s in range(4)]
+                    else:
+                        at = [(2 * s + xx) * 80 + dy * 8 for s in range(4)]
+                        rows = [even[dz, a : a + 64] for a in at]
+                    parts.append(jnp.concatenate(rows, axis=0))
+        left = jnp.concatenate(parts, axis=1)
+        return jnp.dot(left, right[half], preferred_element_type=jnp.float32)
+
+    wait_halo(halo_copies)
+
+    def child_half(b, carry):
+        pad(b, pool_c)
+        acc[b] = product(0)
+        return carry
+
+    lax.fori_loop(0, count, child_half, 0)
+
+    for copy in skip_copies:
+        copy.wait_recv()
+    mine[1].wait()
+    for b in range(count):
+        whole[b] = recv_s[sources[1][b]].astype(jnp.float32)
+        faces(b, pool_s)
+    skip_halo = send_halo(pool_s, halo_s, 1)
+    wait_halo(skip_halo)
+
+    def skip_half(b, carry):
+        pad(b, pool_s)
+        total = jnp.maximum(acc[b] + product(1), 0.0).astype(result.dtype)
+        for s in range(4):
+            for p in range(2):
+                at = (2 * s + p) * 64
+                result[b, at : at + 64] = total[s * 64 : s * 64 + 64, p * made : (p + 1) * made]
+        pltpu.make_async_copy(result.at[b], out_hbm.at[b], outs.at[b]).start()
+        return carry
+
+    lax.fori_loop(0, count, skip_half, 0)
+
+    for copy in mark_copies + parent_copies + skip_copies:
+        copy.wait_send()
+    finish_halo(halo_copies)
+    finish_halo(skip_halo)
+    for copy in agree_copies:
+        copy.wait()
+    for x in range(n_gx):
+        enough = lax.min(enough, agrees[x, 0])
+    agreed[0] = enough
+    for b in range(count):
+        pltpu.make_async_copy(result.at[b], out_hbm.at[b], outs.at[b]).wait()
+
+
 META = 8
-VMEM_LIMIT = 60 * 2**20
 
 
 def vmem():
     return pl.BlockSpec(memory_space=pltpu.VMEM)
-
-
-def smem():
-    return pl.BlockSpec(memory_space=pltpu.SMEM)
-
-
-def anywhere():
-    return pl.BlockSpec(memory_space=pl.ANY)
 
 
 def pack_kernel(
@@ -140,7 +586,7 @@
             pltpu.SemaphoreType.DMA((2, gy_count)),
             pltpu.SemaphoreType.DMA((2,)),
         ],
-        compiler_params=pltpu.CompilerParams(collective_id=0, has_side_effects=True),
+        compiler_params=pltpu.CompilerParams(collective_id=2, has_side_effects=True),
         name="exchange",
     )(in_p, in_s)
 
@@ -441,7 +887,7 @@
     )(near, feats, own, before, after, conv_weight)
 
 
-def per_device(parents, parent_dest, skip, skip_dest, neighbours, up_weight, conv_weight):
+def general(parents, parent_dest, skip, skip_dest, neighbours, up_weight, conv_weight):
     bricks_dev = neighbours.shape[0]
     gy_count = lax.axis_size("gy")
     sent_p, sent_s = pack(parent_dest, skip_dest, parents, skip, bricks_dev, gy_count)
@@ -456,6 +902,75 @@
     flat = (-1,) + faces.shape[2:]
     before, after = halo(to_before.reshape(flat), to_after.reshape(flat))
     return refine(neighbours, feats, faces.reshape(flat), before, after, conv_weight)
+
+
+def per_device(parents, parent_dest, skip, skip_dest, neighbours, up_weight, conv_weight):
+    count = neighbours.shape[0]
+    n_gx, n_gy = lax.axis_size("gx"), lax.axis_size("gy")
+    voxels = skip.shape[1]
+    made = conv_weight.shape[2]
+    bf16, f32 = jnp.bfloat16, jnp.float32
+    pool = (8 * count + 1, 64, made)
+    dma = pltpu.SemaphoreType.DMA
+    refined, agreed = pl.pallas_call(
+        functools.partial(kernel, n_gx, n_gy),
+        out_shape=(
+            jax.ShapeDtypeStruct((count, voxels, made), bf16),
+            jax.ShapeDtypeStruct((1,), jnp.int32),
+        ),
+        in_specs=[smem(), smem(), smem()] + [anywhere()] * 4,
+        out_specs=(anywhere(), smem()),
+        scratch_shapes=[
+            pltpu.VMEM(parents.shape, bf16),
+            pltpu.VMEM(skip.shape, bf16),
+            pltpu.VMEM(up_weight.shape, bf16),
+            pltpu.VMEM(conv_weight.shape, bf16),
+            pltpu.VMEM((n_gy,) + parents.shape[1:], bf16),
+            pltpu.VMEM((n_gy,) + skip.shape[1:], bf16),
+            pltpu.VMEM((n_gy,) + parents.shape[1:], bf16),
+            pltpu.VMEM((n_gy,) + skip.shape[1:], bf16),
+            pltpu.SMEM((2 * n_gy + 1,), jnp.int32),
+            pltpu.SMEM((n_gy, 2 * n_gy + 1), jnp.int32),
+            pltpu.SMEM((1,), jnp.int32),
+            pltpu.SMEM((n_gx, 1), jnp.int32),
+            pltpu.SMEM((2 * count,), jnp.int32),
+            pltpu.SMEM((26 * count,), jnp.int32),
+            pltpu.VMEM((4, 128, 128), f32),
+            pltpu.VMEM((count, voxels, made), f32),
+            pltpu.VMEM((4, 64, made), f32),
+            pltpu.VMEM((6 * count, 64, made), bf16),
+            pltpu.VMEM(pool, bf16),
+            pltpu.VMEM(pool, bf16),
+            pltpu.VMEM((2, count, 64, made), bf16),
+            pltpu.VMEM((2, count, 64, made), bf16),
+            pltpu.VMEM((100 * PITCH, made), f32),
+            pltpu.VMEM((3, 800, made), bf16),
+            pltpu.VMEM((3, 640, made), bf16),
+            pltpu.VMEM((2, 36 * made, 2 * made), bf16),
+            pltpu.VMEM((count, voxels // 2, 2 * made), f32),
+            pltpu.VMEM((count, voxels, made), bf16),
+            dma((4,)),
+            dma((3, n_gy)),
+            dma((3, n_gy)),
+            dma((2, 2)),
+            dma((2, 2)),
+            dma((2,)),
+            dma((count,)),
+            dma((n_gx,)),
+            dma((n_gx,)),
+        ],
+        compiler_params=pltpu.CompilerParams(
+            collective_id=0, has_side_effects=True, vmem_limit_bytes=VMEM_LIMIT
+        ),
+        name="refine_level",
+    )(parent_dest, skip_dest, neighbours, parents, skip, up_weight, conv_weight)
+    return lax.cond(
+        agreed[0] > 0,
+        lambda: refined,
+        lambda: general(
+            parents, parent_dest, skip, skip_dest, neighbours, up_weight, conv_weight
+        ),
+    )
 
 
 def solution(mesh):

time: 69.9 us -> 48.6 us (0.70)
  the two profiles are of different devices: /device:TPU:1 before, /device:TPU:4 now
where the time goes in v2:
time: 48.6 us; the launch traced here: 48.4 us
  Pallas kernels  45.8 us (94%)
  local copies, waits for them, and re-layouts  1.88 us (4%)
  between operations  0.67 us (1%)
    pallas_call x1, Pallas kernels, per_device(): pl.pallas_call(functools.partial(kernel, n_gx, n_gy), out_shape=(jax.Shap...  45.8 us
    unnamed x5, local copies, waits for them, and re-layouts  1.88 us

profile of v2, /device:TPU:4, one launch (start us, length us, event | category | flops | bytes accessed | tf_op | source)
XLA Modules:
  0.0 48.4 jit_solution(13914243443679886469)
XLA Ops:
  0.0 0.0 copy-start
  0.0 0.0 copy-start.1
  0.0 45.8 %refine_level.1 = (bf16[4,512,128]{2,1,0:T(8,128)(2,1)}, s32[1]{0:T(128)}) custom-call(s32[8]{0:T(128)} %pdest.1, s32[8]{0:T(128)} %sdest.1, s32[4,26]{1,0:T(4,128)} %near.1, bf16[8,64,256]{2,1,0:T(8,128)(2,1)} %parents_hbm.1, bf16[8,512,128]{2,1,0:T(8,128)(2,1)} %skip_hbm.1, bf16[8,256,128]{2,1,0:T(8,128)(2,1)} %up_hbm.1, bf16[27,256,128]{2,1,0:T(8,128)(2,1)} %conv_hbm.1), custom_call_target="tpu_custom_call" | custom-call | tf_op jit(solution)/shard_map/refine_level/pallas_call | solution.py:915
  46.5 0.0 copy-done
  46.5 0.0 copy-done.1
  46.5 1.9 %copy.13 = bf16[4,512,128]{2,1,0:T(8,128)(2,1)} copy(bf16[4,512,128]{2,1,0:T(8,128)(2,1)} %get-tuple-element.44) | data formatting | bytes 1048576
  (1 shorter events, 0.0 us)
Async XLA Ops:
  0.0 46.5 %copy-start = (bf16[27,256,128]{2,1,0:T(8,128)(2,1)S(1)}, bf16[27,256,128]{2,1,0:T(8,128)(2,1)}, u32[]{:S(2)}) copy-start(bf16[27,256,128]{2,1,0:T(8,128)(2,1)} %conv_hbm.1) | copy-start | bytes 5308420
  0.0 46.5 %copy-start.1 = (bf16[8,64,256]{2,1,0:T(8,128)(2,1)S(1)}, bf16[8,64,256]{2,1,0:T(8,128)(2,1)}, u32[]{:S(2)}) copy-start(bf16[8,64,256]{2,1,0:T(8,128)(2,1)} %parents_hbm.1) | copy-start | bytes 786436

commit v3 on v2

--- a/solution.py
+++ b/solution.py
@@ -14,7 +14,8 @@
     for x, y, z in steps
 ]
 PITCH = 24
-VMEM_LIMIT = 62 * 2**20
+VMEM_LIMIT = 24 * 2**20
+SHELL, INSIDE = 296, 216
 MESH = pl.DeviceIdType.MESH
 
 
@@ -33,6 +34,25 @@
             other = other + bit * (1 - 2 * lax.rem(lax.div(me, bit), 2))
         bit *= 2
     return other
+
+
+def column(u, v):
+    return (u * 10 + v) * PITCH
+
+
+def product(even, odd, right):
+    parts = []
+    for xx in range(4):
+        for dy in range(3):
+            for dz in range(3):
+                if dy == 1:
+                    rows = [odd[dz, (2 * s + xx) * 64 : (2 * s + xx) * 64 + 64] for s in range(4)]
+                else:
+                    at = [(2 * s + xx) * 80 + dy * 8 for s in range(4)]
+                    rows = [even[dz, a : a + 64] for a in at]
+                parts.append(jnp.concatenate(rows, axis=0))
+    left = jnp.concatenate(parts, axis=1)
+    return jnp.dot(left, right[...], preferred_element_type=jnp.float32)
 
 
 def kernel(
@@ -45,18 +65,28 @@
     skip_hbm,
     up_hbm,
     conv_hbm,
-    out_hbm,
+    acc,
+    even_s,
+    odd_s,
+    right_s,
     agreed,
     parents,
     skip,
     up,
     conv,
     stage_p,
-    stage_s,
+    stage_shell,
+    stage_inside,
     recv_p,
-    recv_s,
+    recv_shell,
+    recv_inside,
     marks,
     land,
+    chosen,
+    flag,
+    flags,
+    wide,
+    strip,
     agree,
     agrees,
     face_pick,
@@ -70,18 +100,16 @@
     halo_c,
     halo_s,
     body,
+    body_s,
     even,
     odd,
     right,
-    acc,
-    result,
     loads,
     sends,
     receives,
     halo_sends,
     halo_receives,
     own_copy,
-    outs,
     agree_sends,
     agree_receives,
 ):
@@ -133,13 +161,11 @@
             barrier, inc=1, device_id={"gx": lax.rem(gx + step, n_gx)}, device_id_type=MESH
         )
 
-    picks = []
     for which, dest in enumerate((pdest, sdest)):
         targets = [dest[s] for s in range(slots)]
         owners = [
             jnp.where(t >= 0, lax.rem(lax.div(lax.max(t, 0), count), n_gy), -1) for t in targets
         ]
-        picked = []
         for d in range(n_gy):
             slot, mark = jnp.int32(0), jnp.int32(-1)
             for s in range(slots):
@@ -147,15 +173,66 @@
                 slot = jnp.where(here, s, slot)
                 mark = jnp.where(here, targets[s], mark)
             marks[which * n_gy + d] = mark
-            picked.append(slot)
-        picks.append(picked)
+            chosen[which * n_gy + d] = slot
 
     load[0].wait()
     for d in range(n_gy):
-        stage_p[d] = parents[picks[0][d]]
+        stage_p[d] = parents[chosen[d]]
     load[1].wait()
-    for d in range(n_gy):
-        stage_s[d] = skip[picks[1][d]]
+
+    def split(d, carry):
+        wide[...] = skip[chosen[n_gy + d]].astype(jnp.float32)
+        columns = [wide[0:64], wide[448:512]]
+        for x in range(1, 7):
+            columns += [wide[x * 64 : x * 64 + 8], wide[x * 64 + 56 : x * 64 + 64]]
+        stage_shell[d, 0:224] = jnp.concatenate(columns, axis=0).astype(stage_shell.dtype)
+        for i in range(12):
+            z, x = i // 6 * 7, i % 6 + 1
+            strip[6 * i : 6 * i + 8] = wide[pl.ds(x * 64 + 8 + z, 8, stride=8), :]
+        stage_shell[d, 224:304] = strip[0:80].astype(stage_shell.dtype)
+        for i in range(36):
+            at = (i // 6 + 1) * 64 + (i % 6 + 1) * 8 + 1
+            strip[80 + 6 * i : 88 + 6 * i] = wide[at : at + 8]
+        stage_inside[d] = strip[80:304].astype(stage_inside.dtype)
+        return carry
+
+    lax.fori_loop(0, n_gy, split, 0)
+
+    pl.semaphore_wait(
+        barrier, n_gx + n_gy - 2 + wraps_ahead.astype(jnp.int32) + wraps_behind.astype(jnp.int32)
+    )
+
+    def remote(source, landing, kind, step):
+        return pltpu.make_async_remote_copy(
+            src_ref=source,
+            dst_ref=landing,
+            send_sem=sends.at[kind, step],
+            recv_sem=receives.at[kind, step],
+            device_id={"gy": partner(me, step)},
+            device_id_type=MESH,
+        )
+
+    mark_copies = [remote(marks, land.at[me], 0, s) for s in order]
+    parent_copies = [remote(stage_p.at[partner(me, s)], recv_p.at[me], 1, s) for s in order]
+    shell_copies, inside_copies = [
+        [remote(stage.at[partner(me, s), pl.ds(0, size)], recv.at[me, pl.ds(0, size)], kind, s) for s in order]
+        for kind, stage, recv, size in (
+            (2, stage_shell, recv_shell, SHELL),
+            (3, stage_inside, recv_inside, INSIDE),
+        )
+    ]
+    flag_copies = [remote(flag, flags.at[me], 4, s) for s in order]
+    mine = [
+        pltpu.make_async_copy(stage.at[me], recv.at[me], own_copy.at[i])
+        for i, (stage, recv) in enumerate(
+            ((stage_p, recv_p), (stage_shell, recv_shell), (stage_inside, recv_inside))
+        )
+    ]
+    early = max(1, len(cross) // 2)
+    for copy in mark_copies + parent_copies + shell_copies[:early] + mine:
+        copy.start()
+    for i in range(2 * n_gy):
+        land[me, i] = marks[i]
 
     last = 8 * count
 
@@ -181,49 +258,22 @@
             spots[b * 26 + k] = lax.min(lax.max(spot, 0), last)
         return enough
 
-    marks[2 * n_gy] = lax.fori_loop(0, count, tables, jnp.int32(1))
-
-    pl.semaphore_wait(
-        barrier, n_gx + n_gy - 2 + wraps_ahead.astype(jnp.int32) + wraps_behind.astype(jnp.int32)
-    )
-
-    def remote(source, landing, kind, step):
-        return pltpu.make_async_remote_copy(
-            src_ref=source,
-            dst_ref=landing,
-            send_sem=sends.at[kind, step],
-            recv_sem=receives.at[kind, step],
-            device_id={"gy": partner(me, step)},
-            device_id_type=MESH,
-        )
-
-    mark_copies = [remote(marks, land.at[me], 0, s) for s in order]
-    parent_copies = [remote(stage_p.at[partner(me, s)], recv_p.at[me], 1, s) for s in order]
-    skip_copies = [remote(stage_s.at[partner(me, s)], recv_s.at[me], 2, s) for s in order]
-    mine = [
-        pltpu.make_async_copy(stage_p.at[me], recv_p.at[me], own_copy.at[0]),
-        pltpu.make_async_copy(stage_s.at[me], recv_s.at[me], own_copy.at[1]),
-    ]
-    early = max(1, len(cross) // 2)
-    for copy in mark_copies + parent_copies + skip_copies[:early] + mine:
+    flag[0] = lax.fori_loop(0, count, tables, jnp.int32(1))
+    for copy in flag_copies:
         copy.start()
-    for i in range(2 * n_gy + 1):
-        land[me, i] = marks[i]
+    flags[me, 0] = flag[0]
+
 
     for copy in load[2:]:
         copy.wait()
     zero = jnp.zeros((made, made), conv.dtype)
-    for half in range(2):
+    for half, into in enumerate((right, right_s)):
         rows = slice(half * made, (half + 1) * made)
         for xx in range(4):
             for yz in range(9):
                 at = (xx * 9 + yz) * made
-                right[half, at : at + made, 0:made] = (
-                    conv[xx * 9 + yz, rows, :] if xx < 3 else zero
-                )
-                right[half, at : at + made, made:] = (
-                    conv[(xx - 1) * 9 + yz, rows, :] if xx > 0 else zero
-                )
+                into[at : at + made, 0:made] = conv[xx * 9 + yz, rows, :] if xx < 3 else zero
+                into[at : at + made, made:] = conv[(xx - 1) * 9 + yz, rows, :] if xx > 0 else zero
     for pool in (pool_c, pool_s):
         pool[last] = jnp.zeros(pool.shape[1:], pool.dtype)
     spread[...] = jnp.zeros_like(spread)
@@ -231,24 +281,6 @@
     for copy in mark_copies + parent_copies:
         copy.wait_recv()
     mine[0].wait()
-    enough = land[0, 2 * n_gy]
-    for d in range(1, n_gy):
-        enough = lax.min(enough, land[d, 2 * n_gy])
-    agree[0] = enough
-    agrees[gx, 0] = enough
-    agree_copies = [
-        pltpu.make_async_remote_copy(
-            src_ref=agree,
-            dst_ref=agrees.at[gx],
-            send_sem=agree_sends.at[step],
-            recv_sem=agree_receives.at[step],
-            device_id={"gx": lax.rem(gx + step, n_gx)},
-            device_id_type=MESH,
-        )
-        for step in range(1, n_gx)
-    ]
-    for copy in agree_copies:
-        copy.start()
     sources = []
     for which in range(2):
         held = [land[d, which * n_gy + me] for d in range(n_gy)]
@@ -272,6 +304,22 @@
             else:
                 value = whole[b, pl.ds(edge, 64, stride=8), :]
             value = value.astype(pool.dtype)
+            own[b * 6 + f] = value
+            pool[b * 6 + f] = value
+
+    def faces_of_body(b, pool):
+        for f in range(6):
+            edge = 7 * (f % 2)
+            if f < 2:
+                rows = [body_s[b, pl.ds(column(edge + 1, y + 1) + 8, 8), :] for y in range(8)]
+            elif f < 4:
+                rows = [body_s[b, pl.ds(column(x + 1, edge + 1) + 8, 8), :] for x in range(8)]
+            else:
+                rows = [
+                    body_s[b, pl.ds(column(x + 1, 1) + 8 + edge, 8, stride=PITCH), :]
+                    for x in range(8)
+                ]
+            value = jnp.concatenate(rows, axis=0).astype(pool.dtype)
             own[b * 6 + f] = value
             pool[b * 6 + f] = value
 
@@ -348,23 +396,16 @@
         upsample(b, sources[0][b])
         faces(b, pool_c)
     halo_copies = send_halo(pool_c, halo_c, 0)
-    for copy in skip_copies[early:]:
+    for copy in shell_copies[early:] + inside_copies[:early]:
         copy.start()
 
-    def pad(b, pool):
-        def column(u, v):
-            return (u * 10 + v) * PITCH
-
+    def surround(b, pool, body):
         def taken(step):
             return pool.at[spots[b * 26 + direction_of[step]]]
 
         def part(step, low, high):
             return taken(step)[low:high].astype(jnp.float32)
 
-        for x in range(8):
-            for y in range(8):
-                at = column(x + 1, y + 1) + 8
-                body[at : at + 8] = whole[b, x * 64 + y * 8 : x * 64 + y * 8 + 8]
         for ox in (-1, 1):
             u, ex = (0, 7) if ox < 0 else (9, 0)
             value = part((ox, 0, 0), 0, 64)
@@ -403,6 +444,7 @@
                 body[pl.ds(column(1, v) + z, 8, stride=10 * PITCH), :] = ghost[
                     p * 2 + q, pl.ds(ey, 8, stride=8), :
                 ]
+    def shifts(body, even, odd):
         for dz in range(3):
             for u in range(10):
                 blocks = [
@@ -413,51 +455,77 @@
                     odd.dtype
                 )
 
-    def product(half):
-        parts = []
-        for xx in range(4):
-            for dy in range(3):
-                for dz in range(3):
-                    if dy == 1:
-                        rows = [odd[dz, (2 * s + xx) * 64 : (2 * s + xx) * 64 + 64] for s in range(4)]
-                    else:
-                        at = [(2 * s + xx) * 80 + dy * 8 for s in range(4)]
-                        rows = [even[dz, a : a + 64] for a in at]
-                    parts.append(jnp.concatenate(rows, axis=0))
-        left = jnp.concatenate(parts, axis=1)
-        return jnp.dot(left, right[half], preferred_element_type=jnp.float32)
-
     wait_halo(halo_copies)
 
     def child_half(b, carry):
-        pad(b, pool_c)
-        acc[b] = product(0)
+        for x in range(8):
+            for y in range(8):
+                at = column(x + 1, y + 1) + 8
+                body[at : at + 8] = whole[b, x * 64 + y * 8 : x * 64 + y * 8 + 8]
+        surround(b, pool_c, body)
+        shifts(body, even, odd)
+        acc[b] = product(even, odd, right)
         return carry
 
     lax.fori_loop(0, count, child_half, 0)
 
-    for copy in skip_copies:
+    for copy in shell_copies:
         copy.wait_recv()
     mine[1].wait()
     for b in range(count):
-        whole[b] = recv_s[sources[1][b]].astype(jnp.float32)
-        faces(b, pool_s)
+        outer = recv_shell[sources[1][b]].astype(jnp.float32)
+        padded = body_s.at[b]
+        for y in range(8):
+            padded[column(1, y + 1) + 8 : column(1, y + 1) + 16] = outer[y * 8 : y * 8 + 8]
+            padded[column(8, y + 1) + 8 : column(8, y + 1) + 16] = outer[64 + y * 8 : 72 + y * 8]
+        for x in range(1, 7):
+            at = 112 + x * 16
+            padded[column(x + 1, 1) + 8 : column(x + 1, 1) + 16] = outer[at : at + 8]
+            padded[column(x + 1, 8) + 8 : column(x + 1, 8) + 16] = outer[at + 8 : at + 16]
+        strip[0:80] = outer[224:304]
+        for i in range(12):
+            at = column(i % 6 + 2, 2) + 8 + i // 6 * 7
+            padded[pl.ds(at, 6, stride=PITCH), :] = strip[6 * i : 6 * i + 6]
+        faces_of_body(b, pool_s)
     skip_halo = send_halo(pool_s, halo_s, 1)
+    for copy in inside_copies[early:]:
+        copy.start()
+    for copy in flag_copies:
+        copy.wait_recv()
+    enough = flags[0, 0]
+    for d in range(1, n_gy):
+        enough = lax.min(enough, flags[d, 0])
+    agree[0] = enough
+    agrees[gx, 0] = enough
+    agree_copies = [
+        pltpu.make_async_remote_copy(
+            src_ref=agree,
+            dst_ref=agrees.at[gx],
+            send_sem=agree_sends.at[step],
+            recv_sem=agree_receives.at[step],
+            device_id={"gx": lax.rem(gx + step, n_gx)},
+            device_id_type=MESH,
+        )
+        for step in range(1, n_gx)
+    ]
+    for copy in agree_copies:
+        copy.start()
     wait_halo(skip_halo)
-
-    def skip_half(b, carry):
-        pad(b, pool_s)
-        total = jnp.maximum(acc[b] + product(1), 0.0).astype(result.dtype)
-        for s in range(4):
-            for p in range(2):
-                at = (2 * s + p) * 64
-                result[b, at : at + 64] = total[s * 64 : s * 64 + 64, p * made : (p + 1) * made]
-        pltpu.make_async_copy(result.at[b], out_hbm.at[b], outs.at[b]).start()
-        return carry
-
-    lax.fori_loop(0, count, skip_half, 0)
-
-    for copy in mark_copies + parent_copies + skip_copies:
+    for b in range(count):
+        surround(b, pool_s, body_s.at[b])
+
+    for copy in inside_copies:
+        copy.wait_recv()
+    mine[2].wait()
+    for b in range(count):
+        padded = body_s.at[b]
+        strip[80:304] = recv_inside[sources[1][b]].astype(jnp.float32)
+        for i in range(36):
+            at = column(i // 6 + 2, i % 6 + 2) + 9
+            padded[at : at + 6] = strip[80 + 6 * i : 86 + 6 * i]
+        shifts(padded, even_s.at[b], odd_s.at[b])
+
+    for copy in mark_copies + parent_copies + shell_copies + inside_copies + flag_copies:
         copy.wait_send()
     finish_halo(halo_copies)
     finish_halo(skip_halo)
@@ -466,8 +534,38 @@
     for x in range(n_gx):
         enough = lax.min(enough, agrees[x, 0])
     agreed[0] = enough
-    for b in range(count):
-        pltpu.make_async_copy(result.at[b], out_hbm.at[b], outs.at[b]).wait()
+
+def finish_kernel(acc, even, odd, right, out, result, sems):
+    copies = []
+    for b in range(acc.shape[0]):
+        made = acc.shape[2] // 2
+        total = acc[b] + product(even.at[b], odd.at[b], right)
+        total = jnp.maximum(total, 0.0).astype(result.dtype)
+        for s in range(4):
+            for p in range(2):
+                at = (2 * s + p) * 64
+                result[b, at : at + 64] = total[s * 64 : s * 64 + 64, p * made : (p + 1) * made]
+        copies.append(pltpu.make_async_copy(result.at[b], out.at[b], sems.at[b]))
+        copies[-1].start()
+    for copy in copies:
+        copy.wait()
+
+
+def finish(acc, even, odd, right):
+    count, made = acc.shape[0], acc.shape[2] // 2
+    shape = (count, 2 * acc.shape[1], made)
+    return pl.pallas_call(
+        finish_kernel,
+        out_shape=pltpu.HBM(shape, jnp.bfloat16),
+        in_specs=[vmem()] * 4,
+        out_specs=pl.BlockSpec(memory_space=pltpu.HBM),
+        scratch_shapes=[
+            pltpu.VMEM(shape, jnp.bfloat16),
+            pltpu.SemaphoreType.DMA((count,)),
+        ],
+        compiler_params=pltpu.CompilerParams(vmem_limit_bytes=24 * 2**20),
+        name="finish",
+    )(acc, even, odd, right)
 
 
 META = 8
@@ -586,7 +684,9 @@
             pltpu.SemaphoreType.DMA((2, gy_count)),
             pltpu.SemaphoreType.DMA((2,)),
         ],
-        compiler_params=pltpu.CompilerParams(collective_id=2, has_side_effects=True),
+        compiler_params=pltpu.CompilerParams(
+            collective_id=2, has_side_effects=True, vmem_limit_bytes=2**20
+        ),
         name="exchange",
     )(in_p, in_s)
 
@@ -660,7 +760,9 @@
         in_specs=[anywhere(), anywhere()],
         out_specs=(anywhere(), anywhere()),
         scratch_shapes=[pltpu.SemaphoreType.DMA((2,)), pltpu.SemaphoreType.DMA((2,))],
-        compiler_params=pltpu.CompilerParams(collective_id=1, has_side_effects=True),
+        compiler_params=pltpu.CompilerParams(
+            collective_id=1, has_side_effects=True, vmem_limit_bytes=2**20
+        ),
         name="halo",
     )(to_before, to_after)
 
@@ -912,25 +1014,36 @@
     bf16, f32 = jnp.bfloat16, jnp.float32
     pool = (8 * count + 1, 64, made)
     dma = pltpu.SemaphoreType.DMA
-    refined, agreed = pl.pallas_call(
+    width = 2 * made
+    acc, even, odd, right, agreed = pl.pallas_call(
         functools.partial(kernel, n_gx, n_gy),
         out_shape=(
-            jax.ShapeDtypeStruct((count, voxels, made), bf16),
+            pltpu.VMEM((count, voxels // 2, width), f32),
+            pltpu.VMEM((count, 3, 800, made), bf16),
+            pltpu.VMEM((count, 3, 640, made), bf16),
+            pltpu.VMEM((36 * made, width), bf16),
             jax.ShapeDtypeStruct((1,), jnp.int32),
         ),
         in_specs=[smem(), smem(), smem()] + [anywhere()] * 4,
-        out_specs=(anywhere(), smem()),
+        out_specs=(vmem(), vmem(), vmem(), vmem(), smem()),
         scratch_shapes=[
             pltpu.VMEM(parents.shape, bf16),
             pltpu.VMEM(skip.shape, bf16),
             pltpu.VMEM(up_weight.shape, bf16),
             pltpu.VMEM(conv_weight.shape, bf16),
             pltpu.VMEM((n_gy,) + parents.shape[1:], bf16),
-            pltpu.VMEM((n_gy,) + skip.shape[1:], bf16),
+            pltpu.VMEM((n_gy, 304, skip.shape[2]), bf16),
+            pltpu.VMEM((n_gy, 224, skip.shape[2]), bf16),
             pltpu.VMEM((n_gy,) + parents.shape[1:], bf16),
-            pltpu.VMEM((n_gy,) + skip.shape[1:], bf16),
-            pltpu.SMEM((2 * n_gy + 1,), jnp.int32),
-            pltpu.SMEM((n_gy, 2 * n_gy + 1), jnp.int32),
+            pltpu.VMEM((n_gy, 304, skip.shape[2]), bf16),
+            pltpu.VMEM((n_gy, 224, skip.shape[2]), bf16),
+            pltpu.SMEM((2 * n_gy,), jnp.int32),
+            pltpu.SMEM((n_gy, 2 * n_gy), jnp.int32),
+            pltpu.SMEM((2 * n_gy,), jnp.int32),
+            pltpu.SMEM((1,), jnp.int32),
+            pltpu.SMEM((n_gy, 1), jnp.int32),
+            pltpu.VMEM((voxels, skip.shape[2]), f32),
+            pltpu.VMEM((304, skip.shape[2]), f32),
             pltpu.SMEM((1,), jnp.int32),
             pltpu.SMEM((n_gx, 1), jnp.int32),
             pltpu.SMEM((2 * count,), jnp.int32),
@@ -944,32 +1057,32 @@
             pltpu.VMEM((2, count, 64, made), bf16),
             pltpu.VMEM((2, count, 64, made), bf16),
             pltpu.VMEM((100 * PITCH, made), f32),
+            pltpu.VMEM((count, 100 * PITCH, made), f32),
             pltpu.VMEM((3, 800, made), bf16),
             pltpu.VMEM((3, 640, made), bf16),
-            pltpu.VMEM((2, 36 * made, 2 * made), bf16),
-            pltpu.VMEM((count, voxels // 2, 2 * made), f32),
-            pltpu.VMEM((count, voxels, made), bf16),
+            pltpu.VMEM((36 * made, width), bf16),
             dma((4,)),
-            dma((3, n_gy)),
-            dma((3, n_gy)),
+            dma((5, n_gy)),
+            dma((5, n_gy)),
             dma((2, 2)),
             dma((2, 2)),
-            dma((2,)),
-            dma((count,)),
+            dma((3,)),
             dma((n_gx,)),
             dma((n_gx,)),
         ],
         compiler_params=pltpu.CompilerParams(
-            collective_id=0, has_side_effects=True, vmem_limit_bytes=VMEM_LIMIT
+            collective_id=0, has_side_effects=True, vmem_limit_bytes=40 * 2**20
         ),
         name="refine_level",
     )(parent_dest, skip_dest, neighbours, parents, skip, up_weight, conv_weight)
-    return lax.cond(
-        agreed[0] > 0,
-        lambda: refined,
-        lambda: general(
-            parents, parent_dest, skip, skip_dest, neighbours, up_weight, conv_weight
-        ),
+    return lax.switch(
+        agreed[0],
+        [
+            lambda: general(
+                parents, parent_dest, skip, skip_dest, neighbours, up_weight, conv_weight
+            ),
+            lambda: finish(acc, even, odd, right),
+        ],
     )
 
 

time: 48.6 us -> 45.3 us (0.932)
  the two profiles are of different devices: /device:TPU:4 before, /device:TPU:0 now
where the time goes in v3:
time: 45.3 us; the launch traced here: 45.1 us
  Pallas kernels  44.4 us (98%)
  between operations  0.65 us (1%)
    pallas_call x1, Pallas kernels, per_device(): pl.pallas_call(functools.partial(kernel, n_gx, n_gy), out_shape=(pltpu.VM...  41.1 us
    pallas_call x1, Pallas kernels, finish(): pl.pallas_call(finish_kernel, out_shape=pltpu.HBM(shape, jnp.bfloat16), i...  3.33 us

profile of v3, /device:TPU:0, one launch (start us, length us, event | category | flops | bytes accessed | tf_op | source)
XLA Modules:
  0.0 45.1 jit_solution(3028662462928400868)
XLA Ops:
  0.0 0.0 copy-start
  0.0 0.0 copy-start.2
  0.0 0.0 copy-start.4
  0.0 0.0 copy-start.6
  0.0 0.0 copy-start.1
  0.0 0.0 copy-start.5
  0.0 0.0 copy-start.3
  0.0 41.1 %refine_level.1 = (f32[4,256,256]{2,1,0:T(8,128)S(1)}, bf16[4,3,800,128]{3,2,1,0:T(8,128)(2,1)S(1)}, bf16[4,3,640,128]{3,2,1,0:T(8,128)(2,1)S(1)}, bf16[4608,256]{1,0:T(8,128)(2,1)S(1)}, s32[1]{0:T(128)}) custom-call(s32[8]{0:T(128)} %pdest.1, s32[8]{0:T(128)} %sdest.1, s32[4,26]{1,0:T(4,128)} %near.1, bf16[8,64,256]{2,1,0:T(8,128)(2,1)} %parents_hbm.1, ...), custom_call_target="tpu_custom_call" | custom-call | tf_op jit(solution)/shard_map/refine_level/pallas_call | solution.py:1018
  41.7 0.0 copy-done
  41.7 0.0 copy-done.2
  41.7 0.0 copy-done.4
  41.7 0.0 copy-done.6
  41.7 0.0 copy-done.1
  41.7 0.0 copy-done.5
  41.7 0.0 copy-done.3
  41.7 3.4 %conditional.1 = (bf16[4,512,128]{2,1,0:T(8,128)(2,1)}) conditional(s32[]{:T(128)} %bitcast.3, (s32[8]{0:T(128)S(1)}, s32[8]{0:T(128)S(1)}, bf16[8,64,256]{2,1,0:T(8,128)(2,1)S(1)}, bf16[8,512,128]{2,1,0:T(8,128)(2,1)S(1)}, s32[4,26]{1,0:T(4,128)S(1)}, /*index=5*/bf16[8,256,128]{2,1,0:T(8,128)(2,1)S(1)}, ...), branch_computations={%region_0.2_spmd, %region_2.3_spmd} | conditional | flops 248 | bytes 264 | solution.py:1078
  41.8 3.3 %finish.1 = bf16[4,512,128]{2,1,0:T(8,128)(2,1)} custom-call(f32[4,256,256]{2,1,0:T(8,128)S(1)} %get-tuple-element.47.acc, bf16[4,3,800,128]{3,2,1,0:T(8,128)(2,1)S(1)} %get-tuple-element.48.even, bf16[4,3,640,128]{3,2,1,0:T(8,128)(2,1)S(1)} %get-tuple-element.49.odd, bf16[4608,256]{1,0:T(8,128)(2,1)S(1)} %get-tuple-element.50.right), custom_call_target="tpu_custom_call" | custom-call | tf_op jit(solution)/shard_map/cond/branch_1_fun/finish/pallas_call | solution.py:557
Async XLA Ops:
  0.0 41.7 %copy-start = (bf16[27,256,128]{2,1,0:T(8,128)(2,1)S(1)}, bf16[27,256,128]{2,1,0:T(8,128)(2,1)}, u32[]{:S(2)}) copy-start(bf16[27,256,128]{2,1,0:T(8,128)(2,1)} %conv_hbm.1) | copy-start | bytes 5308420
  0.0 41.7 %copy-start.2 = (bf16[8,256,128]{2,1,0:T(8,128)(2,1)S(1)}, bf16[8,256,128]{2,1,0:T(8,128)(2,1)}, u32[]{:S(2)}) copy-start(bf16[8,256,128]{2,1,0:T(8,128)(2,1)} %up_hbm.1) | copy-start | bytes 1572868
  0.0 41.7 %copy-start.4 = (s32[4,26]{1,0:T(4,128)S(1)}, s32[4,26]{1,0:T(4,128)}, u32[]{:S(2)}) copy-start(s32[4,26]{1,0:T(4,128)} %near.1) | copy-start | bytes 1252
  0.0 41.7 %copy-start.6 = (s32[8]{0:T(128)S(1)}, s32[8]{0:T(128)}, u32[]{:S(2)}) copy-start(s32[8]{0:T(128)} %sdest.1) | copy-start | bytes 100
  0.0 41.7 %copy-start.1 = (bf16[8,512,128]{2,1,0:T(8,128)(2,1)S(1)}, bf16[8,512,128]{2,1,0:T(8,128)(2,1)}, u32[]{:S(2)}) copy-start(bf16[8,512,128]{2,1,0:T(8,128)(2,1)} %skip_hbm.1) | copy-start | bytes 3145732
  0.0 41.7 %copy-start.5 = (s32[8]{0:T(128)S(1)}, s32[8]{0:T(128)}, u32[]{:S(2)}) copy-start(s32[8]{0:T(128)} %pdest.1) | copy-start | bytes 100
  0.0 41.7 %copy-start.3 = (bf16[8,64,256]{2,1,0:T(8,128)(2,1)S(1)}, bf16[8,64,256]{2,1,0:T(8,128)(2,1)}, u32[]{:S(2)}) copy-start(bf16[8,64,256]{2,1,0:T(8,128)(2,1)} %parents_hbm.1) | copy-start | bytes 786436

commit v4 on v3

--- a/solution.py
+++ b/solution.py
@@ -126,9 +126,9 @@
         return (lax.div(device, n_gy), lax.rem(device, n_gy))
 
     ahead, behind = coordinates(flat + 1), coordinates(flat - 1)
-    order = list(range(n_gy - 1, 0, -1))
-    cross = [s for s in order if s >= n_gy // 2]
-    rest = [s for s in order if s < n_gy // 2]
+    cross = list(range(n_gy // 2, n_gy))
+    rest = list(range(2, n_gy // 2)) + [1]
+    order = cross + rest
 
     load = [
         pltpu.make_async_copy(parents_hbm, parents, loads.at[0]),
@@ -396,7 +396,7 @@
         upsample(b, sources[0][b])
         faces(b, pool_c)
     halo_copies = send_halo(pool_c, halo_c, 0)
-    for copy in shell_copies[early:] + inside_copies[:early]:
+    for copy in shell_copies[early:] + inside_copies:
         copy.start()
 
     def surround(b, pool, body):
@@ -488,8 +488,6 @@
             padded[pl.ds(at, 6, stride=PITCH), :] = strip[6 * i : 6 * i + 6]
         faces_of_body(b, pool_s)
     skip_halo = send_halo(pool_s, halo_s, 1)
-    for copy in inside_copies[early:]:
-        copy.start()
     for copy in flag_copies:
         copy.wait_recv()
     enough = flags[0, 0]

time: 45.3 us -> 43.4 us (0.958)
  the two profiles are of different devices: /device:TPU:0 before, /device:TPU:1 now
where the time goes in v4:
time: 43.4 us; the launch traced here: 43.2 us
  Pallas kernels  42.5 us (98%)
  between operations  0.66 us (2%)
    pallas_call x1, Pallas kernels, per_device(): pl.pallas_call(functools.partial(kernel, n_gx, n_gy), out_shape=(pltpu.VM...  39.2 us
    pallas_call x1, Pallas kernels, finish(): pl.pallas_call(finish_kernel, out_shape=pltpu.HBM(shape, jnp.bfloat16), i...  3.33 us

profile of v4, /device:TPU:1, one launch (start us, length us, event | category | flops | bytes accessed | tf_op | source)
XLA Modules:
  0.0 43.2 jit_solution(15196767589574116608)
XLA Ops:
  0.0 0.0 copy-start
  0.0 0.0 copy-start.2
  0.0 0.0 copy-start.4
  0.0 0.0 copy-start.6
  0.0 0.0 copy-start.1
  0.0 0.0 copy-start.5
  0.0 0.0 copy-start.3
  0.0 39.2 %refine_level.1 = (f32[4,256,256]{2,1,0:T(8,128)S(1)}, bf16[4,3,800,128]{3,2,1,0:T(8,128)(2,1)S(1)}, bf16[4,3,640,128]{3,2,1,0:T(8,128)(2,1)S(1)}, bf16[4608,256]{1,0:T(8,128)(2,1)S(1)}, s32[1]{0:T(128)}) custom-call(s32[8]{0:T(128)} %pdest.1, s32[8]{0:T(128)} %sdest.1, s32[4,26]{1,0:T(4,128)} %near.1, bf16[8,64,256]{2,1,0:T(8,128)(2,1)} %parents_hbm.1, ...), custom_call_target="tpu_custom_call" | custom-call | tf_op jit(solution)/shard_map/refine_level/pallas_call | solution.py:1016
  39.8 0.0 copy-done
  39.8 0.0 copy-done.2
  39.8 0.0 copy-done.4
  39.8 0.0 copy-done.6
  39.8 0.0 copy-done.1
  39.8 0.0 copy-done.5
  39.8 0.0 copy-done.3
  39.8 3.4 %conditional.1 = (bf16[4,512,128]{2,1,0:T(8,128)(2,1)}) conditional(s32[]{:T(128)} %bitcast.3, (s32[8]{0:T(128)S(1)}, s32[8]{0:T(128)S(1)}, bf16[8,64,256]{2,1,0:T(8,128)(2,1)S(1)}, bf16[8,512,128]{2,1,0:T(8,128)(2,1)S(1)}, s32[4,26]{1,0:T(4,128)S(1)}, /*index=5*/bf16[8,256,128]{2,1,0:T(8,128)(2,1)S(1)}, ...), branch_computations={%region_0.2_spmd, %region_2.3_spmd} | conditional | flops 248 | bytes 264 | solution.py:1076
  39.9 3.3 %finish.1 = bf16[4,512,128]{2,1,0:T(8,128)(2,1)} custom-call(f32[4,256,256]{2,1,0:T(8,128)S(1)} %get-tuple-element.47.acc, bf16[4,3,800,128]{3,2,1,0:T(8,128)(2,1)S(1)} %get-tuple-element.48.even, bf16[4,3,640,128]{3,2,1,0:T(8,128)(2,1)S(1)} %get-tuple-element.49.odd, bf16[4608,256]{1,0:T(8,128)(2,1)S(1)} %get-tuple-element.50.right), custom_call_target="tpu_custom_call" | custom-call | tf_op jit(solution)/shard_map/cond/branch_1_fun/finish/pallas_call | solution.py:555
Async XLA Ops:
  0.0 39.8 %copy-start = (bf16[27,256,128]{2,1,0:T(8,128)(2,1)S(1)}, bf16[27,256,128]{2,1,0:T(8,128)(2,1)}, u32[]{:S(2)}) copy-start(bf16[27,256,128]{2,1,0:T(8,128)(2,1)} %conv_hbm.1) | copy-start | bytes 5308420
  0.0 39.8 %copy-start.2 = (bf16[8,256,128]{2,1,0:T(8,128)(2,1)S(1)}, bf16[8,256,128]{2,1,0:T(8,128)(2,1)}, u32[]{:S(2)}) copy-start(bf16[8,256,128]{2,1,0:T(8,128)(2,1)} %up_hbm.1) | copy-start | bytes 1572868
  0.0 39.8 %copy-start.4 = (s32[4,26]{1,0:T(4,128)S(1)}, s32[4,26]{1,0:T(4,128)}, u32[]{:S(2)}) copy-start(s32[4,26]{1,0:T(4,128)} %near.1) | copy-start | bytes 1252
  0.0 39.8 %copy-start.6 = (s32[8]{0:T(128)S(1)}, s32[8]{0:T(128)}, u32[]{:S(2)}) copy-start(s32[8]{0:T(128)} %sdest.1) | copy-start | bytes 100
  0.0 39.8 %copy-start.1 = (bf16[8,512,128]{2,1,0:T(8,128)(2,1)S(1)}, bf16[8,512,128]{2,1,0:T(8,128)(2,1)}, u32[]{:S(2)}) copy-start(bf16[8,512,128]{2,1,0:T(8,128)(2,1)} %skip_hbm.1) | copy-start | bytes 3145732
  0.0 39.8 %copy-start.5 = (s32[8]{0:T(128)S(1)}, s32[8]{0:T(128)}, u32[]{:S(2)}) copy-start(s32[8]{0:T(128)} %pdest.1) | copy-start | bytes 100
  0.0 39.8 %copy-start.3 = (bf16[8,64,256]{2,1,0:T(8,128)(2,1)S(1)}, bf16[8,64,256]{2,1,0:T(8,128)(2,1)}, u32[]{:S(2)}) copy-start(bf16[8,64,256]{2,1,0:T(8,128)(2,1)} %parents_hbm.1) | copy-start | bytes 786436

commit v5 on v4

--- a/solution.py
+++ b/solution.py
@@ -58,9 +58,9 @@
 def kernel(
     n_gx,
     n_gy,
-    pdest,
-    sdest,
-    near,
+    pdest_hbm,
+    sdest_hbm,
+    near_hbm,
     parents_hbm,
     skip_hbm,
     up_hbm,
@@ -70,6 +70,9 @@
     odd_s,
     right_s,
     agreed,
+    pdest,
+    sdest,
+    near,
     parents,
     skip,
     up,
@@ -83,6 +86,7 @@
     marks,
     land,
     chosen,
+    origin,
     flag,
     flags,
     wide,
@@ -130,36 +134,43 @@
     rest = list(range(2, n_gy // 2)) + [1]
     order = cross + rest
 
+    barrier = pltpu.get_barrier_semaphore()
+    wraps_ahead = has_ahead & (me == n_gy - 1)
+    wraps_behind = has_behind & (me == 0)
+
+    @pl.when(wraps_ahead)
+    def _():
+        pl.semaphore_signal(barrier, inc=1, device_id=ahead, device_id_type=MESH)
+
+    @pl.when(wraps_behind)
+    def _():
+        pl.semaphore_signal(barrier, inc=1, device_id=behind, device_id_type=MESH)
+
+    for step in order:
+        pl.semaphore_signal(
+            barrier, inc=1, device_id={"gy": partner(me, step)}, device_id_type=MESH
+        )
+
+    for step in range(1, n_gx):
+        pl.semaphore_signal(
+            barrier, inc=1, device_id={"gx": lax.rem(gx + step, n_gx)}, device_id_type=MESH
+        )
+
     load = [
         pltpu.make_async_copy(parents_hbm, parents, loads.at[0]),
         pltpu.make_async_copy(skip_hbm, skip, loads.at[1]),
         pltpu.make_async_copy(up_hbm, up, loads.at[2]),
         pltpu.make_async_copy(conv_hbm, conv, loads.at[3]),
     ]
-    for copy in load:
+    tables_in = [
+        pltpu.make_async_copy(pdest_hbm, pdest, loads.at[4]),
+        pltpu.make_async_copy(sdest_hbm, sdest, loads.at[5]),
+        pltpu.make_async_copy(near_hbm, near, loads.at[6]),
+    ]
+    for copy in tables_in + load:
         copy.start()
-
-    barrier = pltpu.get_barrier_semaphore()
-    wraps_ahead = has_ahead & (me == n_gy - 1)
-    wraps_behind = has_behind & (me == 0)
-
-    @pl.when(wraps_ahead)
-    def _():
-        pl.semaphore_signal(barrier, inc=1, device_id=ahead, device_id_type=MESH)
-
-    @pl.when(wraps_behind)
-    def _():
-        pl.semaphore_signal(barrier, inc=1, device_id=behind, device_id_type=MESH)
-
-    for step in order:
-        pl.semaphore_signal(
-            barrier, inc=1, device_id={"gy": partner(me, step)}, device_id_type=MESH
-        )
-
-    for step in range(1, n_gx):
-        pl.semaphore_signal(
-            barrier, inc=1, device_id={"gx": lax.rem(gx + step, n_gx)}, device_id_type=MESH
-        )
+    for copy in tables_in:
+        copy.wait()
 
     for which, dest in enumerate((pdest, sdest)):
         targets = [dest[s] for s in range(slots)]
@@ -267,13 +278,17 @@
     for copy in load[2:]:
         copy.wait()
     zero = jnp.zeros((made, made), conv.dtype)
-    for half, into in enumerate((right, right_s)):
-        rows = slice(half * made, (half + 1) * made)
-        for xx in range(4):
-            for yz in range(9):
-                at = (xx * 9 + yz) * made
-                into[at : at + made, 0:made] = conv[xx * 9 + yz, rows, :] if xx < 3 else zero
-                into[at : at + made, made:] = conv[(xx - 1) * 9 + yz, rows, :] if xx > 0 else zero
+
+    def arrange(yz, carry):
+        for half, into in enumerate((right, right_s)):
+            rows = slice(half * made, (half + 1) * made)
+            for xx in range(4):
+                at = pl.ds(pl.multiple_of((xx * 9 + yz) * made, made), made)
+                into[at, 0:made] = conv[xx * 9 + yz, rows, :] if xx < 3 else zero
+                into[at, made:] = conv[(xx - 1) * 9 + yz, rows, :] if xx > 0 else zero
+        return carry
+
+    lax.fori_loop(0, 9, arrange, 0)
     for pool in (pool_c, pool_s):
         pool[last] = jnp.zeros(pool.shape[1:], pool.dtype)
     spread[...] = jnp.zeros_like(spread)
@@ -281,16 +296,13 @@
     for copy in mark_copies + parent_copies:
         copy.wait_recv()
     mine[0].wait()
-    sources = []
     for which in range(2):
         held = [land[d, which * n_gy + me] for d in range(n_gy)]
-        of = []
         for b in range(count):
             source = jnp.int32(0)
             for d in range(n_gy):
                 source = jnp.where(held[d] == first + b, d, source)
-            of.append(source)
-        sources.append(of)
+            origin[which * count + b] = source
 
     def faces(b, pool):
         for f in range(6):
@@ -324,9 +336,12 @@
             pool[b * 6 + f] = value
 
     def send_halo(pool, halo, kind):
-        for b in range(count):
+        def pack_halo(b, carry):
             for side in range(2):
                 halo[side, b] = own[b * 6 + face_pick[b * 2 + side]]
+            return carry
+
+        lax.fori_loop(0, count, pack_halo, 0)
         down = pltpu.make_async_remote_copy(
             src_ref=halo.at[0],
             dst_ref=pool.at[pl.ds(7 * count, count)],
@@ -376,9 +391,9 @@
         def _():
             down.wait_send()
 
-    def upsample(b, source):
+    def upsample(b, carry):
         for half in range(2):
-            values = recv_p[source, :, half * 128 : (half + 1) * 128].astype(jnp.float32)
+            values = recv_p[origin[b], :, half * 128 : (half + 1) * 128].astype(jnp.float32)
             for c in range(2):
                 spread[c * 2 + half, pl.ds(c, 64, stride=2), :] = values
         rows = jnp.concatenate([spread[p] for p in range(4)], axis=1).astype(jnp.bfloat16)
@@ -392,9 +407,10 @@
                         at = (2 * i + a) * 64 + (2 * j + e) * 8
                         whole[b, at : at + 8] = value[(i * 4 + j) * 8 : (i * 4 + j) * 8 + 8]
 
-    for b in range(count):
-        upsample(b, sources[0][b])
         faces(b, pool_c)
+        return carry
+
+    lax.fori_loop(0, count, upsample, 0)
     halo_copies = send_halo(pool_c, halo_c, 0)
     for copy in shell_copies[early:] + inside_copies:
         copy.start()
@@ -472,8 +488,8 @@
     for copy in shell_copies:
         copy.wait_recv()
     mine[1].wait()
-    for b in range(count):
-        outer = recv_shell[sources[1][b]].astype(jnp.float32)
+    def outer_voxels(b, carry):
+        outer = recv_shell[origin[count + b]].astype(jnp.float32)
         padded = body_s.at[b]
         for y in range(8):
             padded[column(1, y + 1) + 8 : column(1, y + 1) + 16] = outer[y * 8 : y * 8 + 8]
@@ -487,6 +503,9 @@
             at = column(i % 6 + 2, 2) + 8 + i // 6 * 7
             padded[pl.ds(at, 6, stride=PITCH), :] = strip[6 * i : 6 * i + 6]
         faces_of_body(b, pool_s)
+        return carry
+
+    lax.fori_loop(0, count, outer_voxels, 0)
     skip_halo = send_halo(pool_s, halo_s, 1)
     for copy in flag_copies:
         copy.wait_recv()
@@ -509,19 +528,25 @@
     for copy in agree_copies:
         copy.start()
     wait_halo(skip_halo)
-    for b in range(count):
+    def surround_skip(b, carry):
         surround(b, pool_s, body_s.at[b])
+        return carry
+
+    lax.fori_loop(0, count, surround_skip, 0)
 
     for copy in inside_copies:
         copy.wait_recv()
     mine[2].wait()
-    for b in range(count):
+    def inner_voxels(b, carry):
         padded = body_s.at[b]
-        strip[80:304] = recv_inside[sources[1][b]].astype(jnp.float32)
+        strip[80:304] = recv_inside[origin[count + b]].astype(jnp.float32)
         for i in range(36):
             at = column(i // 6 + 2, i % 6 + 2) + 9
             padded[at : at + 6] = strip[80 + 6 * i : 86 + 6 * i]
         shifts(padded, even_s.at[b], odd_s.at[b])
+        return carry
+
+    lax.fori_loop(0, count, inner_voxels, 0)
 
     for copy in mark_copies + parent_copies + shell_copies + inside_copies + flag_copies:
         copy.wait_send()
@@ -1022,9 +1047,12 @@
             pltpu.VMEM((36 * made, width), bf16),
             jax.ShapeDtypeStruct((1,), jnp.int32),
         ),
-        in_specs=[smem(), smem(), smem()] + [anywhere()] * 4,
+        in_specs=[anywhere()] * 7,
         out_specs=(vmem(), vmem(), vmem(), vmem(), smem()),
         scratch_shapes=[
+            pltpu.SMEM(parent_dest.shape, jnp.int32),
+            pltpu.SMEM(skip_dest.shape, jnp.int32),
+            pltpu.SMEM(neighbours.shape, jnp.int32),
             pltpu.VMEM(parents.shape, bf16),
             pltpu.VMEM(skip.shape, bf16),
             pltpu.VMEM(up_weight.shape, bf16),
@@ -1038,6 +1066,7 @@
             pltpu.SMEM((2 * n_gy,), jnp.int32),
             pltpu.SMEM((n_gy, 2 * n_gy), jnp.int32),
             pltpu.SMEM((2 * n_gy,), jnp.int32),
+            pltpu.SMEM((2 * count,), jnp.int32),
             pltpu.SMEM((1,), jnp.int32),
             pltpu.SMEM((n_gy, 1), jnp.int32),
             pltpu.VMEM((voxels, skip.shape[2]), f32),
@@ -1059,7 +1088,7 @@
             pltpu.VMEM((3, 800, made), bf16),
             pltpu.VMEM((3, 640, made), bf16),
             pltpu.VMEM((36 * made, width), bf16),
-            dma((4,)),
+            dma((7,)),
             dma((5, n_gy)),
             dma((5, n_gy)),
             dma((2, 2)),

time: 43.4 us -> 42.6 us (0.982)
  Pallas kernels: 42.5 us -> 41.7 us
    pallas_call x1, Pallas kernels: 39.2 us -> 38.4 us  [per_device(): pl.pallas_call(functools.partial(kernel, n_gx, n_gy), out_shape=(pltpu.VM...]
where the time goes in v5:
time: 42.6 us; the launch traced here: 42.5 us
  Pallas kernels  41.7 us (98%)
  between operations  0.66 us (2%)
    pallas_call x1, Pallas kernels, per_device(): pl.pallas_call(functools.partial(kernel, n_gx, n_gy), out_shape=(pltpu.VM...  38.4 us
    pallas_call x1, Pallas kernels, finish(): pl.pallas_call(finish_kernel, out_shape=pltpu.HBM(shape, jnp.bfloat16), i...  3.33 us

profile of v5, /device:TPU:1, one launch (start us, length us, event | category | flops | bytes accessed | tf_op | source)
XLA Modules:
  0.0 42.5 jit_solution(8546807851775560963)
XLA Ops:
  0.0 0.0 copy-start
  0.0 0.0 copy-start.2
  0.0 0.0 copy-start.4
  0.0 0.0 copy-start.6
  0.0 0.0 copy-start.1
  0.0 0.0 copy-start.5
  0.0 0.0 copy-start.3
  0.0 38.4 %refine_level.1 = (f32[4,256,256]{2,1,0:T(8,128)S(1)}, bf16[4,3,800,128]{3,2,1,0:T(8,128)(2,1)S(1)}, bf16[4,3,640,128]{3,2,1,0:T(8,128)(2,1)S(1)}, bf16[4608,256]{1,0:T(8,128)(2,1)S(1)}, s32[1]{0:T(128)}) custom-call(s32[8]{0:T(128)} %pdest_hbm.1, s32[8]{0:T(128)} %sdest_hbm.1, s32[4,26]{1,0:T(4,128)} %near_hbm.1, bf16[8,64,256]{2,1,0:T(8,128)(2,1)} %parents_hbm.1, ...), custom_call_target="tpu_custom_call" | custom-call | tf_op jit(solution)/shard_map/refine_level/pallas_call | solution.py:1041
  39.0 0.0 copy-done
  39.0 0.0 copy-done.2
  39.0 0.0 copy-done.4
  39.1 0.0 copy-done.6
  39.1 0.0 copy-done.1
  39.1 0.0 copy-done.5
  39.1 0.0 copy-done.3
  39.1 3.4 %conditional.1 = (bf16[4,512,128]{2,1,0:T(8,128)(2,1)}) conditional(s32[]{:T(128)} %bitcast.3, (s32[8]{0:T(128)S(1)}, s32[8]{0:T(128)S(1)}, bf16[8,64,256]{2,1,0:T(8,128)(2,1)S(1)}, bf16[8,512,128]{2,1,0:T(8,128)(2,1)S(1)}, s32[4,26]{1,0:T(4,128)S(1)}, /*index=5*/bf16[8,256,128]{2,1,0:T(8,128)(2,1)S(1)}, ...), branch_computations={%region_0.2_spmd, %region_2.3_spmd} | conditional | flops 248 | bytes 264 | solution.py:1105
  39.1 3.3 %finish.1 = bf16[4,512,128]{2,1,0:T(8,128)(2,1)} custom-call(f32[4,256,256]{2,1,0:T(8,128)S(1)} %get-tuple-element.47.acc, bf16[4,3,800,128]{3,2,1,0:T(8,128)(2,1)S(1)} %get-tuple-element.48.even, bf16[4,3,640,128]{3,2,1,0:T(8,128)(2,1)S(1)} %get-tuple-element.49.odd, bf16[4608,256]{1,0:T(8,128)(2,1)S(1)} %get-tuple-element.50.right), custom_call_target="tpu_custom_call" | custom-call | tf_op jit(solution)/shard_map/cond/branch_1_fun/finish/pallas_call | solution.py:580
Async XLA Ops:
  0.0 39.0 %copy-start = (bf16[27,256,128]{2,1,0:T(8,128)(2,1)S(1)}, bf16[27,256,128]{2,1,0:T(8,128)(2,1)}, u32[]{:S(2)}) copy-start(bf16[27,256,128]{2,1,0:T(8,128)(2,1)} %conv_hbm.1) | copy-start | bytes 5308420
  0.0 39.0 %copy-start.2 = (bf16[8,256,128]{2,1,0:T(8,128)(2,1)S(1)}, bf16[8,256,128]{2,1,0:T(8,128)(2,1)}, u32[]{:S(2)}) copy-start(bf16[8,256,128]{2,1,0:T(8,128)(2,1)} %up_hbm.1) | copy-start | bytes 1572868
  0.0 39.0 %copy-start.4 = (s32[4,26]{1,0:T(4,128)S(1)}, s32[4,26]{1,0:T(4,128)}, u32[]{:S(2)}) copy-start(s32[4,26]{1,0:T(4,128)} %near_hbm.1) | copy-start | bytes 1252
  0.0 39.1 %copy-start.6 = (s32[8]{0:T(128)S(1)}, s32[8]{0:T(128)}, u32[]{:S(2)}) copy-start(s32[8]{0:T(128)} %sdest_hbm.1) | copy-start | bytes 100
  0.0 39.1 %copy-start.1 = (bf16[8,512,128]{2,1,0:T(8,128)(2,1)S(1)}, bf16[8,512,128]{2,1,0:T(8,128)(2,1)}, u32[]{:S(2)}) copy-start(bf16[8,512,128]{2,1,0:T(8,128)(2,1)} %skip_hbm.1) | copy-start | bytes 3145732
  0.0 39.1 %copy-start.5 = (s32[8]{0:T(128)S(1)}, s32[8]{0:T(128)}, u32[]{:S(2)}) copy-start(s32[8]{0:T(128)} %pdest_hbm.1) | copy-start | bytes 100
  0.0 39.1 %copy-start.3 = (bf16[8,64,256]{2,1,0:T(8,128)(2,1)S(1)}, bf16[8,64,256]{2,1,0:T(8,128)(2,1)}, u32[]{:S(2)}) copy-start(bf16[8,64,256]{2,1,0:T(8,128)(2,1)} %parents_hbm.1) | copy-start | bytes 786436

commit v6 on v5

--- a/solution.py
+++ b/solution.py
@@ -239,8 +239,8 @@
             ((stage_p, recv_p), (stage_shell, recv_shell), (stage_inside, recv_inside))
         )
     ]
-    early = max(1, len(cross) // 2)
-    for copy in mark_copies + parent_copies + shell_copies[:early] + mine:
+    far, early = len(cross), max(1, len(cross) * 3 // 4)
+    for copy in mark_copies + parent_copies + shell_copies[far:] + shell_copies[:early] + mine:
         copy.start()
     for i in range(2 * n_gy):
         land[me, i] = marks[i]
@@ -412,7 +412,7 @@
 
     lax.fori_loop(0, count, upsample, 0)
     halo_copies = send_halo(pool_c, halo_c, 0)
-    for copy in shell_copies[early:] + inside_copies:
+    for copy in shell_copies[early:far] + inside_copies[far:] + inside_copies[:far]:
         copy.start()
 
     def surround(b, pool, body):

time: 42.6 us -> 42.5 us (level); the launches traced: 42.5 us -> 41.8 us
  Pallas kernels: 41.7 us -> 41.1 us
    pallas_call x1, Pallas kernels: 38.4 us -> 37.7 us  [per_device(): pl.pallas_call(functools.partial(kernel, n_gx, n_gy), out_shape=(pltpu.VM...]
where the time goes in v6:
time: 42.5 us; the launch traced here: 41.8 us
  Pallas kernels  41.1 us (97%)
  between operations  0.66 us (2%)
    pallas_call x1, Pallas kernels, per_device(): pl.pallas_call(functools.partial(kernel, n_gx, n_gy), out_shape=(pltpu.VM...  37.7 us
    pallas_call x1, Pallas kernels, finish(): pl.pallas_call(finish_kernel, out_shape=pltpu.HBM(shape, jnp.bfloat16), i...  3.33 us

profile of v6, /device:TPU:1, one launch (start us, length us, event | category | flops | bytes accessed | tf_op | source)
XLA Modules:
  0.0 41.8 jit_solution(1733935978357793193)
XLA Ops:
  0.0 0.0 copy-start
  0.0 0.0 copy-start.2
  0.0 0.0 copy-start.4
  0.0 0.0 copy-start.6
  0.0 0.0 copy-start.1
  0.0 0.0 copy-start.5
  0.0 0.0 copy-start.3
  0.0 37.7 %refine_level.1 = (f32[4,256,256]{2,1,0:T(8,128)S(1)}, bf16[4,3,800,128]{3,2,1,0:T(8,128)(2,1)S(1)}, bf16[4,3,640,128]{3,2,1,0:T(8,128)(2,1)S(1)}, bf16[4608,256]{1,0:T(8,128)(2,1)S(1)}, s32[1]{0:T(128)}) custom-call(s32[8]{0:T(128)} %pdest_hbm.1, s32[8]{0:T(128)} %sdest_hbm.1, s32[4,26]{1,0:T(4,128)} %near_hbm.1, bf16[8,64,256]{2,1,0:T(8,128)(2,1)} %parents_hbm.1, ...), custom_call_target="tpu_custom_call" | custom-call | tf_op jit(solution)/shard_map/refine_level/pallas_call | solution.py:1041
  38.3 0.0 copy-done
  38.3 0.0 copy-done.2
  38.4 0.0 copy-done.4
  38.4 0.0 copy-done.6
  38.4 0.0 copy-done.1
  38.4 0.0 copy-done.5
  38.4 0.0 copy-done.3
  38.4 3.4 %conditional.1 = (bf16[4,512,128]{2,1,0:T(8,128)(2,1)}) conditional(s32[]{:T(128)} %bitcast.3, (s32[8]{0:T(128)S(1)}, s32[8]{0:T(128)S(1)}, bf16[8,64,256]{2,1,0:T(8,128)(2,1)S(1)}, bf16[8,512,128]{2,1,0:T(8,128)(2,1)S(1)}, s32[4,26]{1,0:T(4,128)S(1)}, /*index=5*/bf16[8,256,128]{2,1,0:T(8,128)(2,1)S(1)}, ...), branch_computations={%region_0.2_spmd, %region_2.3_spmd} | conditional | flops 248 | bytes 264 | solution.py:1105
  38.4 3.3 %finish.1 = bf16[4,512,128]{2,1,0:T(8,128)(2,1)} custom-call(f32[4,256,256]{2,1,0:T(8,128)S(1)} %get-tuple-element.47.acc, bf16[4,3,800,128]{3,2,1,0:T(8,128)(2,1)S(1)} %get-tuple-element.48.even, bf16[4,3,640,128]{3,2,1,0:T(8,128)(2,1)S(1)} %get-tuple-element.49.odd, bf16[4608,256]{1,0:T(8,128)(2,1)S(1)} %get-tuple-element.50.right), custom_call_target="tpu_custom_call" | custom-call | tf_op jit(solution)/shard_map/cond/branch_1_fun/finish/pallas_call | solution.py:580
Async XLA Ops:
  0.0 38.3 %copy-start = (bf16[27,256,128]{2,1,0:T(8,128)(2,1)S(1)}, bf16[27,256,128]{2,1,0:T(8,128)(2,1)}, u32[]{:S(2)}) copy-start(bf16[27,256,128]{2,1,0:T(8,128)(2,1)} %conv_hbm.1) | copy-start | bytes 5308420
  0.0 38.3 %copy-start.2 = (bf16[8,256,128]{2,1,0:T(8,128)(2,1)S(1)}, bf16[8,256,128]{2,1,0:T(8,128)(2,1)}, u32[]{:S(2)}) copy-start(bf16[8,256,128]{2,1,0:T(8,128)(2,1)} %up_hbm.1) | copy-start | bytes 1572868
  0.0 38.4 %copy-start.4 = (s32[4,26]{1,0:T(4,128)S(1)}, s32[4,26]{1,0:T(4,128)}, u32[]{:S(2)}) copy-start(s32[4,26]{1,0:T(4,128)} %near_hbm.1) | copy-start | bytes 1252
  0.0 38.4 %copy-start.6 = (s32[8]{0:T(128)S(1)}, s32[8]{0:T(128)}, u32[]{:S(2)}) copy-start(s32[8]{0:T(128)} %sdest_hbm.1) | copy-start | bytes 100
  0.0 38.4 %copy-start.1 = (bf16[8,512,128]{2,1,0:T(8,128)(2,1)S(1)}, bf16[8,512,128]{2,1,0:T(8,128)(2,1)}, u32[]{:S(2)}) copy-start(bf16[8,512,128]{2,1,0:T(8,128)(2,1)} %skip_hbm.1) | copy-start | bytes 3145732
  0.0 38.4 %copy-start.5 = (s32[8]{0:T(128)S(1)}, s32[8]{0:T(128)}, u32[]{:S(2)}) copy-start(s32[8]{0:T(128)} %pdest_hbm.1) | copy-start | bytes 100
  0.0 38.4 %copy-start.3 = (bf16[8,64,256]{2,1,0:T(8,128)(2,1)S(1)}, bf16[8,64,256]{2,1,0:T(8,128)(2,1)}, u32[]{:S(2)}) copy-start(bf16[8,64,256]{2,1,0:T(8,128)(2,1)} %parents_hbm.1) | copy-start | bytes 786436
